TPU v7x, 512 devices: a whole 4x4x16 slice. The times are simulated.
512 devices in a mesh: row: 32 (over y, x, core), col: 16 (over z).
Axes of the slice: x: 4, y: 4, z: 16, core: 2. Of those that a mesh axis runs over, the one named last changes fastest.
Arguments:
- slab_blocks: bfloat16 [49152, 8192], P('row', 'col'), may hold values from -6 to 6
- slot_tiles: int32 [192, 16], P('row', 'col'), may hold values from 0 to 7, as said below
- live_counts: int32 [32, 16], P('row', 'col'), may hold values from 1 to 6, as said below
- first_prior: float32 [16384, 256], P(('row', 'col'))
- second_prior: float32 [16384, 256], P(('col', 'row')), may hold values from -6 to 6
- first_test: bfloat16 [16384, 256], P('row'), may hold values from -0.046875 to 0.046875
- second_test: bfloat16 [16384, 256], P('col'), may hold values from -0.046875 to 0.046875
- third_test: bfloat16 [2, 256], replicated, may hold values from -4 to 4
- core_first: bfloat16 [512, 16384], P(None, 'row'), may hold values from -0.046875 to 0.046875
- core_second: bfloat16 [16384, 512], P('col'), may hold values from -0.046875 to 0.046875
- core_third: bfloat16 [512, 2], replicated, may hold values from -4 to 4
Outputs:
- first_sketch: float32 [16384, 256], P(('row', 'col'))
- second_sketch: float32 [16384, 256], P(('col', 'row'))
- third_sketch: float32 [2, 256], replicated
- core_update: float32 [512, 512, 512], P('row', 'col')
- first_basis: float32 [16384, 256], P(('row', 'col'))
Inputs may be any that keep to these rules, and one draw needn't show every extreme that they name: `slot_tiles`: within one region pair the first 6 slots name distinct block positions. `live_counts`: some region pair has all 6 slots live.
All inputs are finite; a program needn't handle non-finite values.
Results may differ from a plain program's by a relative error of at most 0.0029.
Values sent between devices are 32-bit elements; how exact they have to be, the bound alone decides.
A program may use at most 64 MiB of HBM per device.

v0:
```python
import jax
import jax.numpy as jnp
from jax import lax
from jax.sharding import PartitionSpec as P


def in_blocks(array, dim, count):
    lengths = array.shape
    tiles = array.reshape(*lengths[:dim], count, lengths[dim] // count, *lengths[dim + 1 :])
    return jnp.moveaxis(tiles, dim, 0)


def sum_at_owner(array, axis, dim):
    tiles = in_blocks(array, dim, lax.axis_size(axis))
    arrived = lax.all_to_all(tiles, axis, split_axis=0, concat_axis=0, tiled=True)
    return arrived.sum(axis=0)


def from_partner(value, axis, stride):
    mask = 2**stride
    pairs = [(source, source ^ mask) for source in range(lax.axis_size(axis))]
    return lax.ppermute(value, axis, pairs)


def add_rows(target, update, start):
    current = lax.dynamic_slice_in_dim(target, start, update.shape[0], 0)
    return lax.dynamic_update_slice_in_dim(target, current + update, start, 0)


def body(
    slab_blocks,
    slot_tiles,
    live_counts,
    first_prior,
    second_prior,
    first_test,
    second_test,
    third_test,
    core_first,
    core_second,
    core_third,
):
    slab_depth = third_test.shape[0]
    factor = third_test.shape[1]
    tile_size = slab_blocks.shape[1] // slab_depth
    tile_cols = second_test.shape[0] // tile_size
    core_width = core_second.shape[1]
    row_span = first_test.shape[0]
    live_slots = live_counts[0, 0]
    mixed_one = third_test[:, None, :] * second_test[None, :, :]
    mixed_two = first_test[:, None, :] * third_test[None, :, :]

    def open_slot(slot_index):
        block_data = lax.dynamic_slice_in_dim(slab_blocks, slot_index * tile_size, tile_size, 0)
        tile_place = slot_tiles[slot_index, 0]
        row_start = tile_place // tile_cols * tile_size
        col_start = tile_place % tile_cols * tile_size
        return (
            block_data,
            block_data.reshape(tile_size * slab_depth, tile_size),
            row_start,
            col_start,
        )

    def sketch_terms(opened, running):
        block_data, flat_block, row_start, col_start = opened
        first_part, second_part, third_part = running
        left_mix = lax.dynamic_slice_in_dim(mixed_one, col_start, tile_size, 1).reshape(
            slab_depth * tile_size, factor
        )
        right_mix = lax.dynamic_slice_in_dim(mixed_two, row_start, tile_size, 0).reshape(
            tile_size * slab_depth, factor
        )
        first_part = add_rows(
            first_part, jnp.dot(block_data, left_mix, preferred_element_type=jnp.float32), row_start
        )
        second_terms = lax.dot_general(
            flat_block, right_mix, (((0,), (0,)), ((), ())), preferred_element_type=jnp.float32
        )
        second_part = add_rows(second_part, second_terms, col_start)
        across = jnp.dot(
            flat_block,
            lax.dynamic_slice_in_dim(second_test, col_start, tile_size, 0),
            preferred_element_type=jnp.float32,
        )
        weights = lax.dynamic_slice_in_dim(first_test, row_start, tile_size, 0).astype(jnp.float32)
        third_part = third_part + jnp.sum(
            across.reshape(tile_size, slab_depth, factor) * weights[:, None, :], axis=0
        )
        return (first_part, second_part, third_part)

    def core_terms(opened, region):
        block_data, flat_block, row_start, col_start = opened
        projected = jnp.dot(
            flat_block,
            lax.dynamic_slice_in_dim(core_second, col_start, tile_size, 0),
            preferred_element_type=jnp.float32,
        )
        return add_rows(region, projected.reshape(tile_size, slab_depth * core_width), row_start)

    sketch_start = (
        jnp.zeros((row_span, factor), jnp.float32),
        jnp.zeros((second_test.shape[0], factor), jnp.float32),
        jnp.zeros((slab_depth, factor), jnp.float32),
    )
    region_start = jnp.zeros((row_span, slab_depth * core_width), jnp.float32)

    def joint_step(slot_index, running):
        opened = open_slot(slot_index)
        return sketch_terms(opened, running[:3]) + (core_terms(opened, running[3]),)

    first_part, second_part, third_part, region = lax.fori_loop(
        0, live_slots, joint_step, sketch_start + (region_start,)
    )
    first_rows = sum_at_owner(first_part, "col", 0)
    second_rows = sum_at_owner(second_part, "row", 0)
    first_sketch = first_prior + first_rows
    second_sketch = second_prior + second_rows
    core_rows = jnp.dot(
        core_first, region.astype(jnp.bfloat16), preferred_element_type=jnp.float32
    ).reshape(core_width, slab_depth, core_width)
    sectioned = sum_at_owner(core_rows, "row", 0)
    core_share = sum_at_owner(sectioned, "col", 2)
    core_update = jnp.einsum(
        "plq,sl->pqs", core_share, core_third.astype(jnp.float32), precision=lax.Precision.HIGHEST
    )
    gram_part = lax.dot_general(
        first_sketch,
        first_sketch,
        (((0,), (0,)), ((), ())),
        precision=lax.Precision.HIGHEST,
        preferred_element_type=jnp.float32,
    )
    combined = jnp.concatenate([gram_part, third_part], axis=0)
    for bit_level in range(lax.axis_size(("row", "col")).bit_length() - 1):
        combined = combined + from_partner(combined, ("row", "col"), bit_level)
    gram_total = combined[:factor]
    third_sketch = combined[factor:]
    chol_lower = jnp.linalg.cholesky(gram_total)
    first_basis = jax.scipy.linalg.solve_triangular(chol_lower, first_sketch.T, lower=True).T
    return (first_sketch, second_sketch, third_sketch, core_update, first_basis)


def solution(mesh):
    return jax.shard_map(
        body,
        mesh=mesh,
        in_specs=(
            P("row", "col"),
            P("row", "col"),
            P("row", "col"),
            P(("row", "col"), None),
            P(("col", "row"), None),
            P("row", None),
            P("col", None),
            P(),
            P(None, "row"),
            P("col", None),
            P(),
        ),
        out_specs=(
            P(("row", "col"), None),
            P(("col", "row"), None),
            P(),
            P("row", "col", None),
            P(("row", "col"), None),
        ),
        check_vma=False,
    )
```

profile of v0, /device:TPU:1, one launch (start us, length us, event | category | flops | bytes accessed | tf_op | source)
XLA Modules:
  0.0 364.4 jit_solution(4186530943115702801)
XLA Ops:
  0.6 2.2 broadcast_multiply_fusion
  2.8 2.3 broadcast_multiply_fusion.1
  8.7 14.5 %while.19 = (s32[]{:T(128)}, f32[512,256]{1,0:T(8,128)}, f32[1024,256]{1,0:T(8,128)}, f32[2,256]{1,0:T(2,128)S(1)}, f32[512,1024]{1,0:T(8,128)}, /*index=5*/s32[...) while((s32[]{:T(128)}, f32[512,256]{1,0:T(8,128)}, ...), condition=%wide.region_2.3_spmd, body=%wide.region_0.2_spmd.sunk | while | flops 336265248 | bytes 19407552 | solution.py:112
  15.3 2.3 add_dynamic-update-slice_fusion.2
  23.1 83.6 %all-to-all-start = ((f32[16,32,256]{2,1,0:T(8,128)}), f32[16,32,256]{2,1,0:T(8,128)S(1)}, u32[]{:S(2)}, u32[]{:S(2)}) async-start(f32[16,32,256]{2,1,0:T(8,128)} %bitcast.82), calls=%async_computation | async-start | bytes 1048576 | tf_op jit(solution)/shard_map/all_to_all | solution.py:15
  106.8 2.3 convolution_bitcast_fusion
  110.9 4.0 %reshape_reshape.3 = f32[32,16,2,512]{3,2,1,0:T(2,128)} reshape(f32[512,1024]{1,0:T(8,128)} %copy.57) | data formatting | bytes 4194304 | tf_op jit(solution)/shard_map/reshape;reshape | solution.py:9
  115.0 11.2 %all-to-all-done = f32[16,32,256]{2,1,0:T(8,128)S(1)} async-done(((f32[16,32,256]{2,1,0:T(8,128)}), f32[16,32,256]{2,1,0:T(8,128)S(1)}, u32[]{:S(2)}, u32[]{:S(2)}) %all-to-all-start) | async-done | bytes 524320 | tf_op jit(solution)/shard_map/all_to_all | solution.py:15
  126.2 4.4 %all-to-all-start.2 = ((f32[32,16,2,512]{3,2,1,0:T(2,128)}), f32[32,16,2,512]{3,2,1,0:T(2,128)S(1)}, u32[]{:S(2)}, u32[]{:S(2)}) async-start(f32[32,16,2,512]{3,2,1,0:T(2,128)} %reshape_reshape.3), calls=%async_computation.2 | async-start | bytes 4194304 | tf_op jit(solution)/shard_map/all_to_all | solution.py:15
  131.3 2.7 collective-permute-start
  134.0 9.7 %collective-permute-done = f32[258,256]{0,1:T(8,128)S(1)} collective-permute-done((f32[258,256]{0,1:T(8,128)S(1)}, f32[258,256]{0,1:T(8,128)S(1)}, u32[]{:S(2)}, u32[]{:S(2)}) %collective-permute-start) | collective-permute-done | bytes 264224 | tf_op jit(solution)/shard_map/ppermute | solution.py:22
  143.7 3.5 collective-permute-start.1
  147.2 18.3 %collective-permute-done.1 = f32[258,256]{0,1:T(8,128)S(1)} collective-permute-done((f32[258,256]{0,1:T(8,128)S(1)}, f32[258,256]{0,1:T(8,128)S(1)}, u32[]{:S(2)}, u32[]{:S(2)}) %collective-permute-start.1) | collective-permute-done | bytes 264224 | tf_op jit(solution)/shard_map/ppermute | solution.py:22
  165.5 5.8 %collective-permute-start.2 = (f32[258,256]{0,1:T(8,128)S(1)}, f32[258,256]{0,1:T(8,128)S(1)}, u32[]{:S(2)}, u32[]{:S(2)}) collective-permute-start(f32[258,256]{0,1:T(8,128)S(1)} %add.133), channel_id=1, source_target_pairs={{0,4},{1,5},{2,6},{3,7},{4,0},{5,1},{6,2},{7,3},{8,12},{9,13},{10,... | collective-permute-start | bytes 792584 | tf_op jit(solution)/shard_map/ppermute | solution.py:22
  171.3 43.8 %collective-permute-done.2 = f32[258,256]{0,1:T(8,128)S(1)} collective-permute-done((f32[258,256]{0,1:T(8,128)S(1)}, f32[258,256]{0,1:T(8,128)S(1)}, u32[]{:S(2)}, u32[]{:S(2)}) %collective-permute-start.2) | collective-permute-done | bytes 264224 | tf_op jit(solution)/shard_map/ppermute | solution.py:22
  215.2 6.9 %collective-permute-start.3 = (f32[258,256]{0,1:T(8,128)S(1)}, f32[258,256]{0,1:T(8,128)S(1)}, u32[]{:S(2)}, u32[]{:S(2)}) collective-permute-start(f32[258,256]{0,1:T(8,128)S(1)} %add.134), channel_id=1, source_target_pairs={{0,8},{1,9},{2,10},{3,11},{4,12},{5,13},{6,14},{7,15},{8,0},{9,1},... | collective-permute-start | bytes 792584 | tf_op jit(solution)/shard_map/ppermute | solution.py:22
  222.1 7.7 %all-to-all-start.1 = ((f32[32,32,256]{2,1,0:T(8,128)}), f32[32,32,256]{2,1,0:T(8,128)}, u32[]{:S(2)}, u32[]{:S(2)}) async-start(f32[32,32,256]{2,1,0:T(8,128)} %bitcast.6), calls=%async_computation.1 | async-start | bytes 2097152 | tf_op jit(solution)/shard_map/all_to_all | solution.py:15
  229.9 8.8 %collective-permute-done.3 = f32[258,256]{0,1:T(8,128)S(1)} collective-permute-done((f32[258,256]{0,1:T(8,128)S(1)}, f32[258,256]{0,1:T(8,128)S(1)}, u32[]{:S(2)}, u32[]{:S(2)}) %collective-permute-start.3) | collective-permute-done | bytes 264224 | tf_op jit(solution)/shard_map/ppermute | solution.py:22
  238.7 2.4 collective-permute-start.4
  242.5 3.1 collective-permute-start.5
  245.7 9.1 %collective-permute-done.5 = f32[258,256]{0,1:T(8,128)S(1)} collective-permute-done((f32[258,256]{0,1:T(8,128)S(1)}, f32[258,256]{0,1:T(8,128)S(1)}, u32[]{:S(2)}, u32[]{:S(2)}) %collective-permute-start.5) | collective-permute-done | bytes 264224 | tf_op jit(solution)/shard_map/ppermute | solution.py:22
  254.8 4.6 %collective-permute-start.6 = (f32[258,256]{0,1:T(8,128)S(1)}, f32[258,256]{0,1:T(8,128)S(1)}, u32[]{:S(2)}, u32[]{:S(2)}) collective-permute-start(f32[258,256]{0,1:T(8,128)S(1)} %add.137), channel_id=1, source_target_pairs={{0,64},{1,65},{2,66},{3,67},{4,68},{5,69},{6,70},{7,71},{8,72},{9,... | collective-permute-start | bytes 792584 | tf_op jit(solution)/shard_map/ppermute | solution.py:22
  259.4 8.2 %collective-permute-done.6 = f32[258,256]{0,1:T(8,128)S(1)} collective-permute-done((f32[258,256]{0,1:T(8,128)S(1)}, f32[258,256]{0,1:T(8,128)S(1)}, u32[]{:S(2)}, u32[]{:S(2)}) %collective-permute-start.6) | collective-permute-done | bytes 264224 | tf_op jit(solution)/shard_map/ppermute | solution.py:22
  267.7 3.1 collective-permute-start.7
  272.8 14.9 %all-to-all-start.3 = ((f32[16,1,1024]{2,1,0:T(1,128)}), f32[16,1,1024]{2,1,0:T(1,128)S(1)}, u32[]{:S(2)}, u32[]{:S(2)}) async-start(f32[16,1,1024]{2,1,0:T(1,128)} %reshape.97), calls=%async_computation.3 | async-start | bytes 131072 | tf_op jit(solution)/shard_map/all_to_all | solution.py:15
  287.8 4.5 %collective-permute-start.8 = (f32[258,256]{0,1:T(8,128)S(1)}, f32[258,256]{0,1:T(8,128)S(1)}, u32[]{:S(2)}, u32[]{:S(2)}) collective-permute-start(f32[258,256]{0,1:T(8,128)S(1)} %add.139), channel_id=1, source_target_pairs={{0,256},{1,257},{2,258},{3,259},{4,260},{5,261},{6,262},{7,263},{8... | collective-permute-start | bytes 792584 | tf_op jit(solution)/shard_map/ppermute | solution.py:22
  294.3 5.0 %all-to-all-done.3 = f32[16,1,1024]{2,1,0:T(1,128)S(1)} async-done(((f32[16,1,1024]{2,1,0:T(1,128)}), f32[16,1,1024]{2,1,0:T(1,128)S(1)}, u32[]{:S(2)}, u32[]{:S(2)}) %all-to-all-start.3) | async-done | bytes 65568 | tf_op jit(solution)/shard_map/all_to_all | solution.py:15
  302.9 11.7 %cholesky.50 = f32[128,128]{1,0:T(8,128)S(1)} custom-call(f32[128,128]{1,0:T(8,128)S(1)} %cholesky.118), custom_call_target="Cholesky" | custom-call | tf_op jit(solution)/shard_map/jit(cholesky)/cholesky | solution.py:139
  314.7 9.8 %custom-call.15 = f32[1,128,128]{1,2,0:T(8,128)S(1)} custom-call(f32[1,128,128]{2,1,0:T(8,128)S(1)} %get-tuple-element.321), custom_call_target="InvertDiagBlocksLowerTriangular" | custom-call | tf_op jit(solution)/shard_map/jit(cholesky)/cholesky | solution.py:139
  325.0 11.7 %cholesky.105 = f32[128,128]{1,0:T(8,128)S(1)} custom-call(f32[128,128]{1,0:T(8,128)S(1)} %convolution_subtract_fusion), custom_call_target="Cholesky" | custom-call | tf_op jit(solution)/shard_map/jit(cholesky)/cholesky | solution.py:139
  338.8 4.1 %while.20 = (s32[]{:T(128)}, f32[256,256]{1,0:T(8,128)S(1)}, s32[2,2]{1,0:T(2,128)S(1)}, f32[2,128,128]{2,1,0:T(8,128)S(1)}, s32[]{:T(128)}) while((s32[]{:T(128)}, f32[256,256]{1,0:T(8,128)S(1)}, s32[2,2]{1,0:T(2,128)S(1)}, f32[2,128,128]{2,1,0:T(8,128)S(1)}, s32[]{:T(128)}) %tuple.62), condition=%wide.while_cond, body=%wide.while_body.sunk | while | flops 2 | bytes 131181 | solution.py:140
  342.9 19.7 %custom-call.16 = f32[2,128,128]{1,2,0:T(8,128)S(1)} custom-call(f32[2,128,128]{2,1,0:T(8,128)S(1)} %get-tuple-element.186), custom_call_target="InvertDiagBlocksLowerTriangular" | custom-call | tf_op jit(solution)/shard_map/jit(_solve_triangular)/triangular_solve | solution.py:140
  (96 shorter events, 30.2 us)
Async XLA Ops:
  0.6 106.1 %copy-start = (bf16[512,512]{1,0:T(8,128)(2,1)S(1)}, bf16[512,512]{1,0:T(8,128)(2,1)}, u32[]{:S(2)}) copy-start(bf16[512,512]{1,0:T(8,128)(2,1)} %param.21) | copy-start | bytes 1572868
  2.8 5.8 %copy-start.4 = (bf16[512,256]{1,0:T(8,128)(2,1)S(1)}, bf16[512,256]{1,0:T(8,128)(2,1)}, u32[]{:S(2)}) copy-start(bf16[512,256]{1,0:T(8,128)(2,1)} %param.18) | copy-start | bytes 786436
  2.8 5.8 %copy-start.9 = (s32[6,1]{0,1:T(1,128)S(1)}, s32[6,1]{0,1:T(1,128)}, u32[]{:S(2)}) copy-start(s32[6,1]{0,1:T(1,128)} %param.14) | copy-start | bytes 76
  14.5 3.1 copy-start.3
  17.6 3.2 copy-start.1
  21.1 1.4 copy-start.2
  23.1 103.1 %all-to-all-start = ((f32[16,32,256]{2,1,0:T(8,128)}), f32[16,32,256]{2,1,0:T(8,128)S(1)}, u32[]{:S(2)}, u32[]{:S(2)}) async-start(f32[16,32,256]{2,1,0:T(8,128)} %bitcast.82), calls=%async_computation | async-start | bytes 1048576 | tf_op jit(solution)/shard_map/all_to_all | solution.py:15
  115.0 15.8 %copy-start.6 = (f32[32,256]{1,0:T(8,128)S(1)}, f32[32,256]{1,0:T(8,128)}, u32[]{:S(2)}) copy-start(f32[32,256]{1,0:T(8,128)} %param.16) | copy-start | bytes 98308
  126.2 95.9 %all-to-all-start.2 = ((f32[32,16,2,512]{3,2,1,0:T(2,128)}), f32[32,16,2,512]{3,2,1,0:T(2,128)S(1)}, u32[]{:S(2)}, u32[]{:S(2)}) async-start(f32[32,16,2,512]{3,2,1,0:T(2,128)} %reshape_reshape.3), calls=%async_computation.2 | async-start | bytes 4194304 | tf_op jit(solution)/shard_map/all_to_all | solution.py:15
  130.8 231.9 %copy-start.5 = (f32[32,256]{1,0:T(8,128)}, f32[32,256]{1,0:T(8,128)S(1)}, u32[]{:S(2)}) copy-start(f32[32,256]{1,0:T(8,128)S(1)} %add.130) | copy-start | bytes 98308
  131.3 12.3 %collective-permute-start = (f32[258,256]{0,1:T(8,128)S(1)}, f32[258,256]{0,1:T(8,128)S(1)}, u32[]{:S(2)}, u32[]{:S(2)}) collective-permute-start(f32[258,256]{0,1:T(8,128)S(1)} %pad_maximum_fusion), channel_id=1, source_target_pairs={{0,1},{1,0},{2,3},{3,2},{4,5},{5,4},{6,7},{7,6},{8,9},{9,8},{10,11... | collective-permute-start | bytes 792584 | tf_op jit(solution)/shard_map/ppermute | solution.py:22
  143.7 21.8 %collective-permute-start.1 = (f32[258,256]{0,1:T(8,128)S(1)}, f32[258,256]{0,1:T(8,128)S(1)}, u32[]{:S(2)}, u32[]{:S(2)}) collective-permute-start(f32[258,256]{0,1:T(8,128)S(1)} %fusion.20), channel_id=1, source_target_pairs={{0,2},{1,3},{2,0},{3,1},{4,6},{5,7},{6,4},{7,5},{8,10},{9,11},{10,... | collective-permute-start | bytes 792584 | tf_op jit(solution)/shard_map/ppermute | solution.py:22
  165.5 49.6 %collective-permute-start.2 = (f32[258,256]{0,1:T(8,128)S(1)}, f32[258,256]{0,1:T(8,128)S(1)}, u32[]{:S(2)}, u32[]{:S(2)}) collective-permute-start(f32[258,256]{0,1:T(8,128)S(1)} %add.133), channel_id=1, source_target_pairs={{0,4},{1,5},{2,6},{3,7},{4,0},{5,1},{6,2},{7,3},{8,12},{9,13},{10,... | collective-permute-start | bytes 792584 | tf_op jit(solution)/shard_map/ppermute | solution.py:22
  215.2 23.5 %collective-permute-start.3 = (f32[258,256]{0,1:T(8,128)S(1)}, f32[258,256]{0,1:T(8,128)S(1)}, u32[]{:S(2)}, u32[]{:S(2)}) collective-permute-start(f32[258,256]{0,1:T(8,128)S(1)} %add.134), channel_id=1, source_target_pairs={{0,8},{1,9},{2,10},{3,11},{4,12},{5,13},{6,14},{7,15},{8,0},{9,1},... | collective-permute-start | bytes 792584 | tf_op jit(solution)/shard_map/ppermute | solution.py:22
  222.1 50.7 %all-to-all-start.1 = ((f32[32,32,256]{2,1,0:T(8,128)}), f32[32,32,256]{2,1,0:T(8,128)}, u32[]{:S(2)}, u32[]{:S(2)}) async-start(f32[32,32,256]{2,1,0:T(8,128)} %bitcast.6), calls=%async_computation.1 | async-start | bytes 2097152 | tf_op jit(solution)/shard_map/all_to_all | solution.py:15
  238.7 3.8 %collective-permute-start.4 = (f32[258,256]{0,1:T(8,128)S(1)}, f32[258,256]{0,1:T(8,128)S(1)}, u32[]{:S(2)}, u32[]{:S(2)}) collective-permute-start(f32[258,256]{0,1:T(8,128)S(1)} %add.135), channel_id=1, source_target_pairs={{0,16},{1,17},{2,18},{3,19},{4,20},{5,21},{6,22},{7,23},{8,24},{9,... | collective-permute-start | bytes 792584 | tf_op jit(solution)/shard_map/ppermute | solution.py:22
  242.5 12.2 %collective-permute-start.5 = (f32[258,256]{0,1:T(8,128)S(1)}, f32[258,256]{0,1:T(8,128)S(1)}, u32[]{:S(2)}, u32[]{:S(2)}) collective-permute-start(f32[258,256]{0,1:T(8,128)S(1)} %add.136), channel_id=1, source_target_pairs={{0,32},{1,33},{2,34},{3,35},{4,36},{5,37},{6,38},{7,39},{8,40},{9,... | collective-permute-start | bytes 792584 | tf_op jit(solution)/shard_map/ppermute | solution.py:22
  254.8 12.8 %collective-permute-start.6 = (f32[258,256]{0,1:T(8,128)S(1)}, f32[258,256]{0,1:T(8,128)S(1)}, u32[]{:S(2)}, u32[]{:S(2)}) collective-permute-start(f32[258,256]{0,1:T(8,128)S(1)} %add.137), channel_id=1, source_target_pairs={{0,64},{1,65},{2,66},{3,67},{4,68},{5,69},{6,70},{7,71},{8,72},{9,... | collective-permute-start | bytes 792584 | tf_op jit(solution)/shard_map/ppermute | solution.py:22
  267.7 20.1 %collective-permute-start.7 = (f32[258,256]{0,1:T(8,128)S(1)}, f32[258,256]{0,1:T(8,128)S(1)}, u32[]{:S(2)}, u32[]{:S(2)}) collective-permute-start(f32[258,256]{0,1:T(8,128)S(1)} %add.138), channel_id=1, source_target_pairs={{0,128},{1,129},{2,130},{3,131},{4,132},{5,133},{6,134},{7,135},{8... | collective-permute-start | bytes 792584 | tf_op jit(solution)/shard_map/ppermute | solution.py:22
  271.5 22.1 %copy-start.7 = (f32[32,256]{1,0:T(8,128)S(1)}, f32[32,256]{1,0:T(8,128)}, u32[]{:S(2)}) copy-start(f32[32,256]{1,0:T(8,128)} %param.17) | copy-start | bytes 98308
  271.7 29.3 %copy-start.8 = (bf16[512,2]{0,1:T(2,128)(2,1)S(1)}, bf16[512,2]{0,1:T(2,128)(2,1)}, u32[]{:S(2)}) copy-start(bf16[512,2]{0,1:T(2,128)(2,1)} %param.23) | copy-start | bytes 6148
  272.8 26.5 %all-to-all-start.3 = ((f32[16,1,1024]{2,1,0:T(1,128)}), f32[16,1,1024]{2,1,0:T(1,128)S(1)}, u32[]{:S(2)}, u32[]{:S(2)}) async-start(f32[16,1,1024]{2,1,0:T(1,128)} %reshape.97), calls=%async_computation.3 | async-start | bytes 131072 | tf_op jit(solution)/shard_map/all_to_all | solution.py:15
  287.8 14.8 %collective-permute-start.8 = (f32[258,256]{0,1:T(8,128)S(1)}, f32[258,256]{0,1:T(8,128)S(1)}, u32[]{:S(2)}, u32[]{:S(2)}) collective-permute-start(f32[258,256]{0,1:T(8,128)S(1)} %add.139), channel_id=1, source_target_pairs={{0,256},{1,257},{2,258},{3,259},{4,260},{5,261},{6,262},{7,263},{8... | collective-permute-start | bytes 792584 | tf_op jit(solution)/shard_map/ppermute | solution.py:22
where the time goes:
time: 369 us; the launch traced here: 364 us
  starting transfers between devices  147 us (40%)
  waiting for transfers between devices  115 us (31%)
  other arithmetic  65.3 us (18%)
  local copies, waits for them, and re-layouts  19.7 us (5%)
  matrix products  9.97 us (3%)
  loops' own time  4.32 us (1%)
    all_to_all x4, starting transfers between devices, sum_at_owner(): lax.all_to_all(tiles, axis, split_axis=0, concat_axis=0, tiled=True)  111 us
    ppermute x9, waiting for transfers between devices, from_partner(): return lax.ppermute(value, axis, pairs)  99.2 us
    ppermute x9, starting transfers between devices, from_partner(): return lax.ppermute(value, axis, pairs)  36.6 us
    another operation x6, other arithmetic, body(): chol_lower = jnp.linalg.cholesky(gram_total)  34 us
    another operation x3, other arithmetic, body(): jax.scipy.linalg.solve_triangular(chol_lower, first_sketch.T, lower=True)  19.7 us
    all_to_all x4, waiting for transfers between devices, sum_at_owner(): lax.all_to_all(tiles, axis, split_axis=0, concat_axis=0, tiled=True)  16.2 us
  transfers between devices with their start and end apart: 13, of which 9 were waited for; matrix products, arithmetic and copies ran while one was open for 5% of the time, Pallas kernels for 0%

commit v1 on v0

v1 whole, which is shorter than its diff:
```python
import functools

import jax
import jax.numpy as jnp
from jax import lax
from jax.experimental import pallas as pl
from jax.experimental.pallas import tpu as pltpu
from jax.sharding import PartitionSpec as P

F32 = jnp.float32
BF16 = jnp.bfloat16
HIGHEST = lax.Precision.HIGHEST


def in_blocks(array, dim, count):
    lengths = array.shape
    tiles = array.reshape(*lengths[:dim], count, lengths[dim] // count, *lengths[dim + 1 :])
    return jnp.moveaxis(tiles, dim, 0)


def sum_at_owner(array, axis, dim):
    tiles = in_blocks(array, dim, lax.axis_size(axis))
    arrived = lax.all_to_all(tiles, axis, split_axis=0, concat_axis=0, tiled=True)
    return arrived.sum(axis=0)


def dot(a, b, dims=((1,), (0,)), precision=None):
    return lax.dot_general(a, b, (dims, ((), ())), precision=precision, preferred_element_type=F32)


def local_kernel(tiles_ref, live_ref, slab, first_t, second_t, third_t, core_f, core_s, first_o, second_o, third_o, core_o, dense, region):
    tile = slab.shape[1] // 2
    slots = slab.shape[0] // tile
    rows, cols = first_t.shape[0], second_t.shape[0]
    tile_cols = cols // tile
    live = live_ref[0, 0]
    for tr in range(rows // tile):
        for tc in range(tile_cols):
            slot, valid = jnp.int32(0), jnp.int32(0)
            for s in range(slots):
                here = jnp.logical_and(tiles_ref[s, 0] == tr * tile_cols + tc, s < live)
                slot = jnp.where(here, s, slot)
                valid = jnp.where(here, 1, valid)
            block = slab[pl.ds(pl.multiple_of(slot * tile, tile), tile), :]
            block = block * valid.astype(F32).astype(BF16)
            dense[tr * tile : (tr + 1) * tile, tc * tile : (tc + 1) * tile] = block[:, :tile]
            dense[tr * tile : (tr + 1) * tile, cols + tc * tile : cols + (tc + 1) * tile] = block[:, tile:]
    third = third_t[...].astype(F32)
    second = second_t[...]
    first_f = first_t[...].astype(F32)
    first_sum, second_sum = None, None
    width = core_s.shape[1]
    for level in range(2):
        part = dense[:, level * cols : (level + 1) * cols]
        mixed_one = (third[level : level + 1, :] * second.astype(F32)).astype(BF16)
        mixed_two = (first_f * third[level : level + 1, :]).astype(BF16)
        one = dot(part, mixed_one)
        two = dot(part, mixed_two, ((0,), (0,)))
        first_sum = one if level == 0 else first_sum + one
        second_sum = two if level == 0 else second_sum + two
        across = dot(part, second)
        third_o[level : level + 1, :] = jnp.sum(across * first_f, axis=0, keepdims=True)
        region[:, level * width : (level + 1) * width] = dot(part, core_s[...]).astype(BF16)
    first_o[...] = first_sum
    second_o[...] = second_sum
    core_o[...] = dot(core_f[...], region[...])


def local_products(slot_tiles, live_counts, slab, first_t, second_t, third_t, core_f, core_s):
    smem = pl.BlockSpec(memory_space=pltpu.SMEM)
    vmem = pl.BlockSpec(memory_space=pltpu.VMEM)
    rows, cols, factor, width = first_t.shape[0], second_t.shape[0], first_t.shape[1], core_s.shape[1]
    shapes = ((rows, factor), (cols, factor), (2, factor), (core_f.shape[0], 2 * width))
    return pl.pallas_call(
        local_kernel,
        out_shape=[jax.ShapeDtypeStruct(s, F32) for s in shapes],
        in_specs=[smem, smem] + [vmem] * 6,
        out_specs=[vmem] * 4,
        scratch_shapes=[pltpu.VMEM((rows, 2 * cols), BF16), pltpu.VMEM((rows, 2 * width), BF16)],
        compiler_params=pltpu.CompilerParams(vmem_limit_bytes=40 * 2**20),
    )(slot_tiles, live_counts, slab, first_t, second_t, third_t, core_f, core_s)


def eliminate(work, size, wide=32, group=8):
    row_at = lax.broadcasted_iota(jnp.int32, (wide, 128), 0)
    row_full = lax.broadcasted_iota(jnp.int32, (wide, size), 0)
    lane_full = lax.broadcasted_iota(jnp.int32, (wide, size), 1)
    for start in range(0, size, wide):
        panel = work[start : start + wide, :]
        inverse_pivots = jnp.zeros((wide, 128), F32)
        for base in range(0, wide, group):
            columns = [
                jnp.broadcast_to(panel[:, start + base + k : start + base + k + 1], (wide, 128)) for k in range(group)
            ]
            for k in range(group):
                row = base + k
                inverse = 1.0 / jnp.broadcast_to(columns[k][row : row + 1, :], (wide, 128))
                inverse_pivots = jnp.where(row_at == row, inverse, inverse_pivots)
                factor = jnp.where(row_at > row, columns[k] * inverse, 0.0)
                for later in range(k + 1, group):
                    columns[later] = columns[later] - factor * columns[later][row : row + 1, :]
                here = lane_full == start + row
                pivot_row = jnp.where(here[row : row + 1, :], 1.0, panel[row : row + 1, :])
                kept = jnp.where(jnp.logical_and(here, row_full > row), 0.0, panel)
                panel = kept - jnp.concatenate([factor] * (size // 128), axis=1) * pivot_row
        work[start : start + wide, :] = panel
        rest = size - start - wide
        if rest:
            inside = jnp.logical_and(lane_full >= start, lane_full < start + wide)
            unit = jnp.where(lane_full == start + row_full, 1.0, panel)
            unit = jnp.where(jnp.logical_and(inside, lane_full > start + row_full), 0.0, unit)
            scaled = jnp.where(inside, unit, 0.0) * jnp.concatenate([inverse_pivots] * (size // 128), axis=1)
            step = dot(scaled, unit, ((0,), (0,)), HIGHEST)
            below = work[start + wide :, :]
            lane_rest = lax.broadcasted_iota(jnp.int32, (rest, size), 1)
            inside_rest = jnp.logical_and(lane_rest >= start, lane_rest < start + wide)
            change = dot(jnp.where(inside_rest, below, 0.0), step, precision=HIGHEST)
            work[start + wide :, :] = jnp.where(inside_rest, 0.0, below) - change


def basis_kernel(gram, sketch, basis, work):
    size = gram.shape[0]
    work[...] = gram[...]
    eliminate(work, size)
    row = lax.broadcasted_iota(jnp.int32, (size, size), 0)
    lane = lax.broadcasted_iota(jnp.int32, (size, size), 1)
    whole = work[...]
    pivots = jnp.sum(jnp.where(row == lane, whole, 0.0), axis=1, keepdims=True)
    inverse = jnp.where(lane < row, whole, jnp.where(lane == row, 1.0, 0.0)) * lax.rsqrt(pivots)
    basis[...] = dot(sketch[...], inverse, ((1,), (1,)), HIGHEST)


def basis_of(gram, sketch):
    vmem = pl.BlockSpec(memory_space=pltpu.VMEM)
    return pl.pallas_call(
        basis_kernel,
        out_shape=jax.ShapeDtypeStruct(sketch.shape, F32),
        in_specs=[vmem, vmem],
        out_specs=vmem,
        scratch_shapes=[pltpu.VMEM(gram.shape, F32)],
    )(gram, sketch)


def body(slab, slot_tiles, live_counts, first_prior, second_prior, first_t, second_t, third_t, core_f, core_s, core_t):
    factor, width = first_t.shape[1], core_s.shape[1]
    first_part, second_part, third_part, core_rows = local_products(
        slot_tiles, live_counts, slab, first_t, second_t, third_t, core_f, core_s
    )
    first_sketch = first_prior + sum_at_owner(first_part, "col", 0)
    second_sketch = second_prior + sum_at_owner(second_part, "row", 0)
    sectioned = sum_at_owner(core_rows.reshape(-1, 2, width), "row", 0)
    core_share = sum_at_owner(sectioned, "col", 2)
    core_update = jnp.einsum("plq,sl->pqs", core_share, core_t.astype(F32), precision=HIGHEST)
    gram_part = dot(first_sketch, first_sketch, ((0,), (0,)), HIGHEST)
    combined = lax.psum(jnp.concatenate([gram_part, third_part], axis=0), ("row", "col"))
    first_basis = basis_of(combined[:factor], first_sketch)
    return (first_sketch, second_sketch, combined[factor:], core_update, first_basis)


def solution(mesh):
    both, swapped = P(("row", "col"), None), P(("col", "row"), None)
    return jax.shard_map(
        body,
        mesh=mesh,
        in_specs=(
            P("row", "col"), P("row", "col"), P("row", "col"), both, swapped,
            P("row", None), P("col", None), P(), P(None, "row"), P("col", None), P(),
        ),
        out_specs=(both, swapped, P(), P("row", "col", None), both),
        check_vma=False,
    )
```

time: 369 us -> 626 us (1.70)
  waiting for transfers between devices: 115 us -> 501 us
  starting transfers between devices: 147 us -> 26.2 us
  other arithmetic: 65.3 us -> 4.22 us
  blocking collectives: 0 us -> 42.4 us
  Pallas kernels: 0 us -> 18.7 us
  between operations: 2.36 us -> 14.8 us
  matrix products: 9.97 us -> 2.03 us
    psum x0 -> x1, waiting for transfers between devices: none -> 467 us  [body(): lax.psum(jnp.concatenate([gram_part, third_part], axis=0), ('row', 'col'))]
    ppermute x9 -> x0, waiting for transfers between devices: 99.2 us -> none  [from_partner(): return lax.ppermute(value, axis, pairs)]
    all_to_all x4 -> x3, starting transfers between devices: 111 us -> 25.9 us  [sum_at_owner(): lax.all_to_all(tiles, axis, split_axis=0, concat_axis=0, tiled=True)]
    another operation x9 -> x0, other arithmetic: 53.7 us -> none  [the longest x6 34 us: body(): chol_lower = jnp.linalg.cholesky(gram_total)]
    all_to_all x0 -> x1, blocking collectives: none -> 42.4 us  [sum_at_owner(): lax.all_to_all(tiles, axis, split_axis=0, concat_axis=0, tiled=True)]
    ppermute x9 -> x0, starting transfers between devices: 36.6 us -> none  [from_partner(): return lax.ppermute(value, axis, pairs)]
    pallas_call x0 -> x2, Pallas kernels: none -> 18.7 us  [the longest x1 14.6 us: basis_of(): pl.pallas_call(basis_kernel, out_shape=jax.ShapeDtypeStruct(sketch.shape,...]
    all_to_all x4 -> x3, waiting for transfers between devices: 16.2 us -> 33.8 us  [sum_at_owner(): lax.all_to_all(tiles, axis, split_axis=0, concat_axis=0, tiled=True)]
  transfers between devices with their start and end apart: 13 -> 4, of which waited for: 9 -> 3; matrix products, arithmetic and copies ran while one was open for 5% -> 2% of each run, Pallas kernels for 0% -> 2%
where the time goes in v1:
time: 626 us; the launch traced here: 624 us
  waiting for transfers between devices  501 us (80%)
  blocking collectives  42.4 us (7%)
  starting transfers between devices  26.2 us (4%)
  Pallas kernels  18.7 us (3%)
  local copies, waits for them, and re-layouts  14.9 us (2%)
  between operations  14.8 us (2%)
    psum x1, waiting for transfers between devices, body(): lax.psum(jnp.concatenate([gram_part, third_part], axis=0), ('row', 'col'))  467 us
    all_to_all x1, blocking collectives, sum_at_owner(): lax.all_to_all(tiles, axis, split_axis=0, concat_axis=0, tiled=True)  42.4 us
    all_to_all x3, waiting for transfers between devices, sum_at_owner(): lax.all_to_all(tiles, axis, split_axis=0, concat_axis=0, tiled=True)  33.8 us
    all_to_all x3, starting transfers between devices, sum_at_owner(): lax.all_to_all(tiles, axis, split_axis=0, concat_axis=0, tiled=True)  25.9 us
    pallas_call x1, Pallas kernels, basis_of(): pl.pallas_call(basis_kernel, out_shape=jax.ShapeDtypeStruct(sketch.shape,...  14.6 us
  transfers between devices with their start and end apart: 4, of which 3 were waited for; matrix products, arithmetic and copies ran while one was open for 2% of the time, Pallas kernels for 2%

profile of v1, /device:TPU:1, one launch (start us, length us, event | category | flops | bytes accessed | tf_op | source)
XLA Modules:
  0.0 624.2 jit_solution(7672488011696977724)
XLA Ops:
  7.2 0.7 copy.20.tiles_ref
  8.6 1.4 copy-done.1
  10.0 1.2 copy-done.2
  11.2 1.0 copy-done.3
  12.3 1.0 copy-done.4
  13.3 0.9 copy-done.5
  14.3 0.7 copy-done.6
  14.9 4.1 shard_map.146
  19.0 15.8 %all-to-all-start = ((f32[16,32,256]{2,1,0:T(8,128)}), f32[16,32,256]{2,1,0:T(8,128)}, u32[]{:S(2)}, u32[]{:S(2)}) async-start(f32[16,32,256]{2,1,0:T(8,128)} %bitcast), calls=%async_computation | async-start | bytes 1048576 | tf_op jit(solution)/shard_map/all_to_all | solution.py:23
  34.8 2.8 reshape_reshape.3
  37.6 20.2 %all-to-all-done = f32[16,32,256]{2,1,0:T(8,128)} async-done(((f32[16,32,256]{2,1,0:T(8,128)}), f32[16,32,256]{2,1,0:T(8,128)}, u32[]{:S(2)}, u32[]{:S(2)}) %all-to-all-start) | async-done | bytes 524320 | tf_op jit(solution)/shard_map/all_to_all | solution.py:23
  57.9 42.4 %all_to_all.20 = f32[32,16,2,512]{3,2,1,0:T(2,128)S(1)} all-to-all(f32[32,16,2,512]{3,2,1,0:T(2,128)} %reshape_reshape.3), channel_id=1, replica_groups=mesh['row'=32,'col'=16] {'row'}, dimensions={0} | all-to-all | bytes 4194304 | tf_op jit(solution)/shard_map/all_to_all | solution.py:23
  100.3 4.1 all-to-all-start.1
  104.4 1.1 reduce_sum.36
  105.5 0.4 fusion.2
  105.9 0.8 reduce_sum.38
  106.9 0.2 copy.22
  107.1 0.9 reshape.23
  108.0 13.6 %all-to-all-done.1 = f32[32,32,256]{2,1,0:T(8,128)S(1)} async-done(((f32[32,32,256]{2,1,0:T(8,128)}), f32[32,32,256]{2,1,0:T(8,128)S(1)}, u32[]{:S(2)}, u32[]{:S(2)}) %all-to-all-start.1) | async-done | bytes 1048608 | tf_op jit(solution)/shard_map/all_to_all | solution.py:23
  121.5 6.0 all-to-all-start.3
  127.6 0.2 all-reduce.2.cloned.1.call-start
  127.8 0.7 pad_maximum_fusion
  128.6 0.6 add.9
  129.3 467.1 %all-reduce.2.cloned.1.call-done = f32[258,256]{1,0:T(8,128)} async-done(((f32[258,256]{1,0:T(8,128)}), f32[258,256]{1,0:T(8,128)}) %all-reduce.2.cloned.1.call-update) | async-done | bytes 264208 | tf_op jit(solution)/shard_map/psum | solution.py:155
  596.4 1.7 slice.9.gram
  598.1 14.6 %shard_map.147 = f32[32,256]{1,0:T(8,128)} custom-call(f32[256,256]{1,0:T(8,128)} %slice.9.gram, f32[32,256]{1,0:T(8,128)} %copy-done.7), custom_call_target="tpu_custom_call" | custom-call | tf_op jit(solution)/shard_map/pallas_call | solution.py:135
  612.7 1.3 slice.8
  614.0 0.5 broadcast
  614.5 0.8 reduce
  615.3 0.2 reshape.24
  615.6 0.1 reduce_sum.39
  615.7 1.6 fusion
  (20 shorter events, 0.3 us)
Async XLA Ops:
  7.2 608.5 %copy-start = (bf16[512,2]{0,1:T(2,128)(2,1)S(1)}, bf16[512,2]{0,1:T(2,128)(2,1)}, u32[]{:S(2)}) copy-start(bf16[512,2]{0,1:T(2,128)(2,1)} %param.21) | copy-start | bytes 6148
  8.6 1.4 copy-start.1
  10.0 1.2 copy-start.2
  11.2 1.0 copy-start.3
  12.3 1.0 copy-start.4
  13.3 0.9 copy-start.5
  14.3 0.7 copy-start.6
  19.0 38.9 %all-to-all-start = ((f32[16,32,256]{2,1,0:T(8,128)}), f32[16,32,256]{2,1,0:T(8,128)}, u32[]{:S(2)}, u32[]{:S(2)}) async-start(f32[16,32,256]{2,1,0:T(8,128)} %bitcast), calls=%async_computation | async-start | bytes 1048576 | tf_op jit(solution)/shard_map/all_to_all | solution.py:23
  100.2 5.2 copy-start.8
  100.3 21.3 %all-to-all-start.1 = ((f32[32,32,256]{2,1,0:T(8,128)}), f32[32,32,256]{2,1,0:T(8,128)S(1)}, u32[]{:S(2)}, u32[]{:S(2)}) async-start(f32[32,32,256]{2,1,0:T(8,128)} %bitcast.1), calls=%async_computation.1 | async-start | bytes 2097152 | tf_op jit(solution)/shard_map/all_to_all | solution.py:23
  105.5 23.1 %copy-start.7 = (f32[32,256]{1,0:T(8,128)}, f32[32,256]{1,0:T(8,128)S(1)}, u32[]{:S(2)}) copy-start(f32[32,256]{1,0:T(8,128)S(1)} %add.8.sketch) | copy-start | bytes 98308
  106.7 21.9 %copy-start.9 = (f32[32,256]{1,0:T(8,128)S(1)}, f32[32,256]{1,0:T(8,128)}, u32[]{:S(2)}) copy-start(f32[32,256]{1,0:T(8,128)} %param.15) | copy-start | bytes 98308
  121.5 492.5 %all-to-all-start.3 = ((f32[16,1,1024]{2,1,0:T(1,128)}), f32[16,1,1024]{2,1,0:T(1,128)S(1)}, u32[]{:S(2)}, u32[]{:S(2)}) async-start(f32[16,1,1024]{2,1,0:T(1,128)} %reshape.23), calls=%async_computation.3 | async-start | bytes 131072 | tf_op jit(solution)/shard_map/all_to_all | solution.py:23
  127.6 468.8 %all-reduce.2.cloned.1.call-start = ((), (), s32[]{:S(2)}) async-start(), calls=%async_computation.4 | async-start | bytes 540672 | tf_op jit(solution)/shard_map/psum | solution.py:155
Sparse Core Ops, SparseCore 0:
  134.4 461.9 all-reduce.1

commit v2 on v1

v2 whole, which is shorter than its diff:
```python
import functools

import jax
import jax.numpy as jnp
from jax import lax
from jax.experimental import pallas as pl
from jax.experimental.pallas import tpu as pltpu
from jax.sharding import PartitionSpec as P

F32 = jnp.float32
BF16 = jnp.bfloat16
HIGHEST = lax.Precision.HIGHEST


def dot(a, b, dims=((1,), (0,)), precision=None):
    return lax.dot_general(a, b, (dims, ((), ())), precision=precision, preferred_element_type=F32)


MESH = pl.DeviceIdType.MESH
SIDE = 4


def ring_order(count):
    return sorted(range(1, count), key=lambda step: -min(step, count - step))


class Sender:
    def __init__(self, send_sems, recv_sems):
        self.send_sems, self.recv_sems, self.copies = send_sems, recv_sems, []

    def __call__(self, source, target, device):
        at = len(self.copies)
        copy = pltpu.make_async_remote_copy(
            src_ref=source, dst_ref=target, send_sem=self.send_sems.at[at], recv_sem=self.recv_sems.at[at],
            device_id=device, device_id_type=MESH,
        )
        copy.start()
        self.copies.append(copy)
        return copy


def arrive(copies):
    for copy in copies:
        copy.wait_recv()


def sums_kernel(
    tiles_ref, live_ref, slab_h, first_h, second_h, third_h, core_f_h, core_s_h, first_prior, second_prior,
    first_o, second_o, third_o, gram_o, share_o,
    slab, first_t, second_t, third_t, core_f, core_s, dense, region,
    first_v, second_v, core_v, third_v, down, up, second_c, core_c, third_c,
    second_1, core_1, second_2, core_2, third_xy, third_z,
    gram_v, gram_c, gram_xy, gram_own, gram_z, gram_done, pieces, pieces_in,
    load_sems, send_sems, recv_sems,
):
    tile = slab.shape[1] // 2
    slots = slab.shape[0] // tile
    rows, cols = first_t.shape[0], second_t.shape[0]
    tile_cols = cols // tile
    width = core_s.shape[1]
    factor = first_t.shape[1]
    row, z = lax.axis_index("row"), lax.axis_index("col")
    rings = lax.axis_size("col")
    core = row % 2
    chip = row // 2
    y, x = chip // SIDE, chip % SIDE
    chips = SIDE * SIDE

    loads = [
        pltpu.make_async_copy(source, target, load_sems.at[i])
        for i, (source, target) in enumerate(
            ((slab_h, slab), (third_h, third_t), (second_h, second_t), (first_h, first_t), (core_s_h, core_s), (core_f_h, core_f))
        )
    ]
    for load in loads:
        load.start()

    def at_chip(dy, dx):
        return ((((y + dy) % SIDE) * SIDE + (x + dx) % SIDE) * 2 + core, z)

    def at_ring(step):
        return (row, (z + step + rings) % rings)

    partner = (chip * 2 + 1 - core, z)
    offsets = sorted(
        [(dy, dx) for dy in range(SIDE) for dx in range(SIDE) if dy or dx],
        key=lambda o: -(min(o[0], SIDE - o[0]) + min(o[1], SIDE - o[1])),
    )
    barrier = pltpu.get_barrier_semaphore()
    others = [partner] + [at_chip(*o) for o in offsets] + [at_ring(s) for s in range(1, rings)]
    for device in others:
        pl.semaphore_signal(barrier, inc=1, device_id=device, device_id_type=MESH)

    send = Sender(send_sems, recv_sems)
    live = live_ref[0, 0]
    places = (rows // tile) * tile_cols
    weights = [
        [jnp.logical_and(tiles_ref[s, 0] == t, s < live).astype(jnp.int32).astype(F32).astype(BF16) for s in range(slots)]
        for t in range(places)
    ]
    loads[0].wait()

    def place_rows(i, carry):
        blocks = [slab[pl.ds(pl.multiple_of(s * tile + i * 16, 16), 16), :] for s in range(slots)]
        for t in range(places):
            block = blocks[0] * weights[t][0]
            for s in range(1, slots):
                block = block + blocks[s] * weights[t][s]
            tr, tc = t // tile_cols, t % tile_cols
            at = pl.ds(pl.multiple_of(tr * tile + i * 16, 16), 16)
            dense[at, tc * tile : (tc + 1) * tile] = block[:, :tile]
            dense[at, cols + tc * tile : cols + (tc + 1) * tile] = block[:, tile:]
        return carry

    lax.fori_loop(0, tile // 16, place_rows, 0)
    loads[1].wait()
    loads[2].wait()
    third = third_t[...].astype(F32)
    halves = [dense.at[:, level * cols : (level + 1) * cols] for level in range(2)]
    first_sum = None
    for level in range(2):
        mixed = (third[level : level + 1, :] * second_t[...].astype(F32)).astype(BF16)
        term = dot(halves[level][...], mixed)
        first_sum = term if level == 0 else first_sum + term
    span = rows // rings
    first_v[...] = first_sum.reshape(rings, span, factor)
    pl.semaphore_wait(barrier, len(others))

    half = rings // 2
    down_copies = [send(first_v.at[(z + half) % rings], down.at[0], at_ring(-1))]
    up_copies = [send(first_v.at[(z + half - 1) % rings], up.at[0], at_ring(1))]

    def first_step(step):
        down_copies[step - 1].wait_recv()
        down[step - 1] = down[step - 1] + first_v[(z + half + step) % rings]
        down_copies.append(send(down.at[step - 1], down.at[step], at_ring(-1)))
        if step < half - 1:
            up_copies[step - 1].wait_recv()
            up[step - 1] = up[step - 1] + first_v[(z + half - 1 - step + rings) % rings]
            up_copies.append(send(up.at[step - 1], up.at[step], at_ring(1)))

    loads[3].wait()
    second_sum = None
    for level in range(2):
        mixed = (first_t[...].astype(F32) * third[level : level + 1, :]).astype(BF16)
        term = dot(halves[level][...], mixed, ((0,), (0,)))
        second_sum = term if level == 0 else second_sum + term
    second_v[...] = second_sum.reshape(second_v.shape)
    second_swap = send(second_v.at[:, :, 1 - core], second_c, partner)
    for level in range(2):
        across = dot(halves[level][...], second_t[...])
        third_v[0:1, level * factor : (level + 1) * factor] = jnp.sum(across * first_t[...].astype(F32), axis=0, keepdims=True)
    third_swap = send(third_v, third_c.at[core], partner)
    first_step(1)
    loads[4].wait()
    for level in range(2):
        region[:, level * width : (level + 1) * width] = dot(halves[level][...], core_s[...]).astype(BF16)
    loads[5].wait()
    core_v[...] = dot(core_f[...], region[...]).reshape(core_v.shape)
    core_swap = send(core_v.at[:, :, 1 - core], core_c, partner)
    first_step(2)

    def start_xy(total, landing):
        rows_half = total.shape[2] // 2
        copies = []
        for step in (2, 1, 3):
            to_x, to_y = (x + step) % SIDE, (y + step) % SIDE
            copies.append(send(total.at[:, to_x, 0:rows_half], landing.at[0, step - 1], at_chip(0, step)))
            copies.append(send(total.at[to_y, :, rows_half:], landing.at[1, step - 1], at_chip(step, 0)))
        return copies

    def middle_xy(total, landing, last):
        rows_half = total.shape[2] // 2
        landing[0, 0] = total[:, x, 0:rows_half] + landing[0, 0] + landing[0, 1] + landing[0, 2]
        landing[1, 0] = total[y, :, rows_half:] + landing[1, 0] + landing[1, 1] + landing[1, 2]
        copies = []
        for step in (2, 1, 3):
            to_x, to_y = (x + step) % SIDE, (y + step) % SIDE
            copies.append(send(landing.at[0, 0, to_y], last.at[0, step - 1], at_chip(step, 0)))
            copies.append(send(landing.at[1, 0, to_x], last.at[1, step - 1], at_chip(0, step)))
        return copies

    second_swap.wait_recv()
    second_c[...] = second_c[...] + second_v[:, :, core]
    second_stage = start_xy(second_c, second_1)
    third_swap.wait_recv()
    third_c[core] = third_v[...]
    third_xy[chip] = third_c[0] + third_c[1]
    third_stage = [send(third_xy.at[chip], third_xy.at[chip], at_chip(*o)) for o in offsets]
    first_step(3)
    core_swap.wait_recv()
    core_c[...] = core_c[...] + core_v[:, :, core]
    core_stage = start_xy(core_c, core_1)
    first_step(4)
    arrive(second_stage)
    second_last = middle_xy(second_c, second_1, second_2)
    arrive(third_stage)
    third_sum = third_xy[0]
    for i in range(1, chips):
        third_sum = third_sum + third_xy[i]
    third_z[z] = third_sum
    third_last = [send(third_z.at[z], third_z.at[z], at_ring(s)) for s in ring_order(rings)]
    first_step(5)
    arrive(core_stage)
    core_last = middle_xy(core_c, core_1, core_2)
    first_step(6)
    arrive(second_last)
    rows_half = second_c.shape[2] // 2
    second_o[0:rows_half, :] = second_prior[0:rows_half, :] + (second_1[0, 0, y] + second_2[0, 0] + second_2[0, 1] + second_2[0, 2])
    second_o[rows_half:, :] = second_prior[rows_half:, :] + (second_1[1, 0, x] + second_2[1, 0] + second_2[1, 1] + second_2[1, 2])
    first_step(7)
    up_copies[-1].wait_recv()
    sketch = first_prior[...] + first_v[z] + up[half - 2]
    down_copies[-1].wait_recv()
    sketch = sketch + down[half - 1]
    first_o[...] = sketch

    gram_v[...] = dot(sketch, sketch, ((0,), (0,)), HIGHEST).reshape(gram_v.shape)
    gram_swap = send(gram_v.at[1 - core], gram_c, partner)

    arrive(core_last)
    rows_half = core_c.shape[2] // 2
    lane = lax.broadcasted_iota(jnp.int32, (rows_half, 128), 1) // 32
    sums = [
        core_1[0, 0, y] + core_2[0, 0] + core_2[0, 1] + core_2[0, 2],
        core_1[1, 0, x] + core_2[1, 0] + core_2[1, 1] + core_2[1, 2],
    ]
    for group in range(width // 128):
        parts = [sums[k // 2][:, (k % 2) * width + group * 128 : (k % 2) * width + (group + 1) * 128] for k in range(4)]
        for m in range(4):
            piece = None
            for k in range(4):
                shift = (k - m) * 32 % 128
                moved = pltpu.roll(parts[k], shift, 1) if shift else parts[k]
                piece = moved if k == 0 else jnp.where(lane == k, moved, piece)
            pieces[group * 4 + m] = piece

    gram_swap.wait_recv()
    gram_c[...] = gram_c[...] + gram_v[core]
    gram_stage = [
        send(gram_c.at[((y + dy) % SIDE) * SIDE + (x + dx) % SIDE], gram_xy.at[dy * SIDE + dx], at_chip(dy, dx)) for dy, dx in offsets
    ]
    arrive(third_last)
    third_sum = third_z[0]
    for i in range(1, rings):
        third_sum = third_sum + third_z[i]
    third_o[...] = third_sum
    arrive(gram_stage)
    total = gram_c[chip]
    for i in range(1, chips):
        total = total + gram_xy[i]
    gram_own[...] = total
    gram_ring = [send(gram_own, gram_z.at[s], at_ring(s)) for s in ring_order(rings)]
    arrive(gram_ring)
    for i in range(1, rings):
        total = total + gram_z[i]
    gram_done[core, chip] = total
    gram_spread = [send(gram_done.at[core, chip], gram_done.at[core, chip], at_chip(*o)) for o in offsets]
    share_stage = [send(pieces.at[(z + s) % rings], pieces_in.at[s], at_ring(s)) for s in ring_order(rings)]
    arrive(gram_spread)
    gram_back = send(gram_done.at[core], gram_done.at[core], partner)
    arrive(share_stage)
    share = pieces[z]
    for i in range(1, rings):
        share = share + pieces_in[i]
    share_o[...] = share
    gram_back.wait_recv()
    gram_o[...] = gram_done[...].reshape(gram_o.shape)
    for copy in send.copies:
        copy.wait_send()


def all_sums(slot_tiles, live_counts, slab, first_t, second_t, third_t, core_f, core_s, first_prior, second_prior):
    smem, vmem, hbm = (pl.BlockSpec(memory_space=m) for m in (pltpu.SMEM, pltpu.VMEM, pl.ANY))
    rows, cols, factor, width = first_t.shape[0], second_t.shape[0], first_t.shape[1], core_s.shape[1]
    rings = lax.axis_size("col")
    chips = SIDE * SIDE
    owned, high = second_prior.shape[0], core_f.shape[0] // lax.axis_size("row")
    span = rows // rings
    half = rings // 2

    def f32(*shape):
        return pltpu.VMEM(shape, F32)

    scratch = [
        *(pltpu.VMEM(a.shape, BF16) for a in (slab, first_t, second_t, third_t, core_f, core_s)),
        pltpu.VMEM((rows, 2 * cols), BF16), pltpu.VMEM((rows, 2 * width), BF16),
        f32(rings, span, factor), f32(SIDE, SIDE, 2, owned, factor), f32(SIDE, SIDE, 2, high, 2 * width), f32(1, 2 * factor),
        f32(half, span, factor), f32(half - 1, span, factor),
        f32(SIDE, SIDE, owned, factor), f32(SIDE, SIDE, high, 2 * width), f32(2, 1, 2 * factor),
        f32(2, SIDE - 1, SIDE, owned // 2, factor), f32(2, SIDE - 1, SIDE, high // 2, 2 * width),
        f32(2, SIDE - 1, owned // 2, factor), f32(2, SIDE - 1, high // 2, 2 * width),
        f32(chips, 1, 2 * factor), f32(rings, 1, 2 * factor),
        f32(2, chips, 8, factor), f32(chips, 8, factor), f32(chips, 8, factor), f32(8, factor), f32(rings, 8, factor),
        f32(2, chips, 8, factor), f32(rings, 8, 128), f32(rings, 8, 128),
        pltpu.SemaphoreType.DMA((6,)), pltpu.SemaphoreType.DMA((160,)), pltpu.SemaphoreType.DMA((160,)),
    ]
    shapes = (first_prior.shape, second_prior.shape, (1, 2 * factor), (factor, factor), (8, 128))
    return pl.pallas_call(
        sums_kernel,
        out_shape=[jax.ShapeDtypeStruct(s, F32) for s in shapes],
        in_specs=[smem, smem] + [hbm] * 6 + [vmem] * 2,
        out_specs=[vmem] * 5,
        scratch_shapes=scratch,
        compiler_params=pltpu.CompilerParams(collective_id=0, has_side_effects=True, vmem_limit_bytes=60 * 2**20),
    )(slot_tiles, live_counts, slab, first_t, second_t, third_t, core_f, core_s, first_prior, second_prior)


def eliminate(work, size, wide=32, group=8):
    row_at = lax.broadcasted_iota(jnp.int32, (wide, 128), 0)
    row_full = lax.broadcasted_iota(jnp.int32, (wide, size), 0)
    lane_full = lax.broadcasted_iota(jnp.int32, (wide, size), 1)
    for start in range(0, size, wide):
        panel = work[start : start + wide, :]
        inverse_pivots = jnp.zeros((wide, 128), F32)
        for base in range(0, wide, group):
            columns = [
                jnp.broadcast_to(panel[:, start + base + k : start + base + k + 1], (wide, 128)) for k in range(group)
            ]
            for k in range(group):
                row = base + k
                inverse = 1.0 / jnp.broadcast_to(columns[k][row : row + 1, :], (wide, 128))
                inverse_pivots = jnp.where(row_at == row, inverse, inverse_pivots)
                factor = jnp.where(row_at > row, columns[k] * inverse, 0.0)
                for later in range(k + 1, group):
                    columns[later] = columns[later] - factor * columns[later][row : row + 1, :]
                here = lane_full == start + row
                pivot_row = jnp.where(here[row : row + 1, :], 1.0, panel[row : row + 1, :])
                kept = jnp.where(jnp.logical_and(here, row_full > row), 0.0, panel)
                panel = kept - jnp.concatenate([factor] * (size // 128), axis=1) * pivot_row
        work[start : start + wide, :] = panel
        rest = size - start - wide
        if rest:
            inside = jnp.logical_and(lane_full >= start, lane_full < start + wide)
            unit = jnp.where(lane_full == start + row_full, 1.0, panel)
            unit = jnp.where(jnp.logical_and(inside, lane_full > start + row_full), 0.0, unit)
            scaled = jnp.where(inside, unit, 0.0) * jnp.concatenate([inverse_pivots] * (size // 128), axis=1)
            step = dot(scaled, unit, ((0,), (0,)), HIGHEST)
            below = work[start + wide :, :]
            lane_rest = lax.broadcasted_iota(jnp.int32, (rest, size), 1)
            inside_rest = jnp.logical_and(lane_rest >= start, lane_rest < start + wide)
            change = dot(jnp.where(inside_rest, below, 0.0), step, precision=HIGHEST)
            work[start + wide :, :] = jnp.where(inside_rest, 0.0, below) - change


def basis_kernel(gram, sketch, share, core_t, basis, update, work):
    size = gram.shape[0]
    work[...] = gram[...]
    turned = share[...].T
    for p in range(16):
        high, low = divmod(p, 8)
        lower = turned[high * 64 : high * 64 + 32, low : low + 1] * core_t[0:1, :]
        update[p] = lower + turned[high * 64 + 32 : high * 64 + 64, low : low + 1] * core_t[1:2, :]
    eliminate(work, size)
    row = lax.broadcasted_iota(jnp.int32, (size, size), 0)
    lane = lax.broadcasted_iota(jnp.int32, (size, size), 1)
    whole = work[...]
    pivots = jnp.sum(jnp.where(row == lane, whole, 0.0), axis=1, keepdims=True)
    inverse = jnp.where(lane < row, whole, jnp.where(lane == row, 1.0, 0.0)) * lax.rsqrt(pivots)
    basis[...] = dot(sketch[...], inverse, ((1,), (1,)), HIGHEST)


def basis_of(gram, sketch, share, core_t):
    vmem = pl.BlockSpec(memory_space=pltpu.VMEM)
    return pl.pallas_call(
        basis_kernel,
        out_shape=[jax.ShapeDtypeStruct(sketch.shape, F32), jax.ShapeDtypeStruct((16, 32, core_t.shape[1]), F32)],
        in_specs=[vmem] * 4,
        out_specs=[vmem] * 2,
        scratch_shapes=[pltpu.VMEM(gram.shape, F32)],
    )(gram, sketch, share, core_t)


def body(slab, slot_tiles, live_counts, first_prior, second_prior, first_t, second_t, third_t, core_f, core_s, core_t):
    first_sketch, second_sketch, third_sketch, gram, share = all_sums(
        slot_tiles, live_counts, slab, first_t, second_t, third_t, core_f, core_s, first_prior, second_prior
    )
    first_basis, core_update = basis_of(gram, first_sketch, share, core_t.astype(F32).T)
    return (first_sketch, second_sketch, third_sketch.reshape(2, -1), core_update, first_basis)


def solution(mesh):
    both, swapped = P(("row", "col"), None), P(("col", "row"), None)
    return jax.shard_map(
        body,
        mesh=mesh,
        in_specs=(
            P("row", "col"), P("row", "col"), P("row", "col"), both, swapped,
            P("row", None), P("col", None), P(), P(None, "row"), P("col", None), P(),
        ),
        out_specs=(both, swapped, P(), P("row", "col", None), both),
        check_vma=False,
    )
```

time: 626 us -> 92.2 us (0.15)
  waiting for transfers between devices: 501 us -> 0 us
  Pallas kernels: 18.7 us -> 83.4 us
  blocking collectives: 42.4 us -> 0 us
  starting transfers between devices: 26.2 us -> 0 us
  between operations: 14.8 us -> 1.31 us
  local copies, waits for them, and re-layouts: 14.9 us -> 5.19 us
    psum x1 -> x0, waiting for transfers between devices: 467 us -> none  [body(): lax.psum(jnp.concatenate([gram_part, third_part], axis=0), ('row', 'col'))]
    pallas_call x2, Pallas kernels: 18.7 us -> 83.4 us  [the longest x1 68.5 us: all_sums(): pl.pallas_call(sums_kernel, out_shape=[jax.ShapeDtypeStruct(s, F32) for s...]
    all_to_all x1 -> x0, blocking collectives: 42.4 us -> none  [sum_at_owner(): lax.all_to_all(tiles, axis, split_axis=0, concat_axis=0, tiled=True)]
    all_to_all x3 -> x0, waiting for transfers between devices: 33.8 us -> none  [sum_at_owner(): lax.all_to_all(tiles, axis, split_axis=0, concat_axis=0, tiled=True)]
    all_to_all x3 -> x0, starting transfers between devices: 25.9 us -> none  [sum_at_owner(): lax.all_to_all(tiles, axis, split_axis=0, concat_axis=0, tiled=True)]
  transfers between devices with their start and end apart: 4 -> 0, of which waited for: 3 -> 0; matrix products, arithmetic and copies ran while one was open for 2% -> 0% of each run, Pallas kernels for 2% -> 0%
where the time goes in v2:
time: 92.2 us; the launch traced here: 91.8 us
  Pallas kernels  83.4 us (90%)
  local copies, waits for them, and re-layouts  5.19 us (6%)
  other arithmetic  1.91 us (2%)
  between operations  1.31 us (1%)
    pallas_call x1, Pallas kernels, all_sums(): pl.pallas_call(sums_kernel, out_shape=[jax.ShapeDtypeStruct(s, F32) for s...  68.5 us
    pallas_call x1, Pallas kernels, basis_of(): pl.pallas_call(basis_kernel, out_shape=[jax.ShapeDtypeStruct(sketch.shape...  14.9 us
    unnamed x5, local copies, waits for them, and re-layouts  4.08 us

profile of v2, /device:TPU:1, one launch (start us, length us, event | category | flops | bytes accessed | tf_op | source)
XLA Modules:
  0.0 91.8 jit_solution(5561566973888629718)
XLA Ops:
  0.6 1.3 %copy.16.tiles_ref = s32[6,1]{1,0:T(8,128)} copy(s32[6,1]{0,1:T(1,128)} %param.12) | data formatting | bytes 48 | tf_op args[1]
  2.6 0.0 copy-start
  2.6 68.5 %shard_map.146 = (f32[32,256]{1,0:T(8,128)}, f32[32,256]{1,0:T(8,128)}, f32[1,512]{1,0:T(1,128)}, f32[256,256]{1,0:T(8,128)}, f32[8,128]{1,0:T(8,128)}) custom-call(s32[6,1]{1,0:T(8,128)} %copy.16.tiles_ref, s32[1,1]{1,0:T(1,128)S(6)} %copy.19.live_ref, bf16[1536,512]{1,0:T(8,128)(2,1)} %slab_h.1, bf16[512,256]{1,0:T(8,128)(2,1)} %first_h.1, ...), custom_call_target="tpu_custom_call" | custom-call | tf_op jit(solution)/shard_map/pallas_call | solution.py:299
  71.1 0.0 copy-done
  71.2 0.6 convert_bitcast_fusion.core_t
  71.7 14.9 %shard_map.147 = (f32[32,256]{1,0:T(8,128)}, f32[16,32,512]{2,1,0:T(8,128)}) custom-call(f32[256,256]{1,0:T(8,128)} %get-tuple-element.15.gram, f32[32,256]{1,0:T(8,128)} %get-tuple-element.24.sketch, f32[8,128]{1,0:T(8,128)} %get-tuple-element.16.share, f32[2,512]{1,0:T(2,128)} %convert_bitcast_fusion.core_t), custom_call_target="tpu_custom_call" | custom-call | tf_op jit(solution)/shard_map/pallas_call | solution.py:365
  86.6 0.5 broadcast.3
  87.1 1.3 %reduce.3 = f32[512]{0:T(512)S(1)} reduce(f32[1,512]{1,0:T(1,128)} %get-tuple-element.14, f32[]{:T(128)} %broadcast.3), dimensions={0}, to_apply=%get-tuple-element.14.reduce_sub_computation.3 | reduce | bytes 4100 | tf_op jit(solution)/shard_map/pallas_call | solution.py:299
  88.5 0.6 reshape.13
  89.0 1.4 %copy.20 = f32[32,256]{1,0:T(8,128)} copy(f32[32,256]{1,0:T(8,128)} %get-tuple-element.24.sketch) | data formatting | bytes 65536
  90.4 1.4 %copy.21 = f32[32,256]{1,0:T(8,128)} copy(f32[32,256]{1,0:T(8,128)} %get-tuple-element.25) | data formatting | bytes 65536
Async XLA Ops:
  2.6 68.5 %copy-start = (bf16[512,2]{0,1:T(2,128)(2,1)S(1)}, bf16[512,2]{0,1:T(2,128)(2,1)}, u32[]{:S(2)}) copy-start(bf16[512,2]{0,1:T(2,128)(2,1)} %param.21) | copy-start | bytes 6148

commit v3 on v2

v3 whole, which is shorter than its diff:
```python
import functools

import jax
import jax.numpy as jnp
from jax import lax
from jax.experimental import pallas as pl
from jax.experimental.pallas import tpu as pltpu
from jax.sharding import PartitionSpec as P

F32 = jnp.float32
BF16 = jnp.bfloat16
HIGHEST = lax.Precision.HIGHEST


def dot(a, b, dims=((1,), (0,)), precision=None):
    return lax.dot_general(a, b, (dims, ((), ())), precision=precision, preferred_element_type=F32)


MESH = pl.DeviceIdType.MESH
SIDE = 4
CUTS = 2
WIDE = 64
GROUP = 16


def ring_order(count):
    return sorted(range(1, count), key=lambda step: -min(step, count - step))


class Sender:
    def __init__(self, send_sems, recv_sems):
        self.send_sems, self.recv_sems, self.copies = send_sems, recv_sems, []

    def __call__(self, source, target, device):
        at = len(self.copies)
        copy = pltpu.make_async_remote_copy(
            src_ref=source, dst_ref=target, send_sem=self.send_sems.at[at], recv_sem=self.recv_sems.at[at],
            device_id=device, device_id_type=MESH,
        )
        copy.start()
        self.copies.append(copy)
        return copy


def arrive(copies):
    for copy in copies:
        copy.wait_recv()


def sums_kernel(
    tiles_h, live_h, slab_h, first_h, second_h, third_h, core_f_h, core_s_h, first_prior, second_prior,
    first_o, second_o, third_o, gram_o, share_o,
    tiles_ref, live_ref, slab, first_t, second_t, third_t, core_f, core_s, dense, region,
    first_v, second_v, core_v, third_v, down_far, down_near, up_far, up_near, second_c, core_c, third_c,
    second_1, core_1, second_2, core_2, third_xy, third_z,
    gram_v, gram_c, gram_xy, gram_own, gram_z, gram_done, pieces, pieces_in,
    load_sems, send_sems, recv_sems,
):
    tile = slab.shape[1] // 2
    slots = slab.shape[0] // tile
    rows, cols = first_t.shape[0], second_t.shape[0]
    tile_cols = cols // tile
    width = core_s.shape[1]
    factor = first_t.shape[1]
    row, z = lax.axis_index("row"), lax.axis_index("col")
    rings = lax.axis_size("col")
    core = row % 2
    chip = row // 2
    y, x = chip // SIDE, chip % SIDE
    chips = SIDE * SIDE

    loads = [
        pltpu.make_async_copy(source, target, load_sems.at[i])
        for i, (source, target) in enumerate(
            ((slab_h, slab), (third_h, third_t), (second_h, second_t), (core_s_h, core_s), (core_f_h, core_f), (first_h, first_t), (tiles_h, tiles_ref), (live_h, live_ref))
        )
    ]
    for load in loads[6:] + loads[:6]:
        load.start()

    def at_chip(dy, dx):
        return ((((y + dy) % SIDE) * SIDE + (x + dx) % SIDE) * 2 + core, z)

    def at_ring(step):
        return (row, (z + step + rings) % rings)

    partner = (chip * 2 + 1 - core, z)
    offsets = sorted(
        [(dy, dx) for dy in range(SIDE) for dx in range(SIDE) if dy or dx],
        key=lambda o: -(min(o[0], SIDE - o[0]) + min(o[1], SIDE - o[1])),
    )
    barrier = pltpu.get_barrier_semaphore()
    others = [partner] + [at_chip(*o) for o in offsets if not (o[0] and o[1])] + [at_ring(s) for s in (-2, -1, 1, 2)]
    for device in others:
        pl.semaphore_signal(barrier, inc=1, device_id=device, device_id_type=MESH)

    send = Sender(send_sems, recv_sems)
    loads[6].wait()
    loads[7].wait()
    live = live_ref[0, 0]
    places = (rows // tile) * tile_cols
    weights = [
        [jnp.logical_and(tiles_ref[s, 0] == t, s < live).astype(jnp.int32).astype(F32).astype(BF16) for s in range(slots)]
        for t in range(places)
    ]
    loads[0].wait()

    def place_rows(i, carry):
        blocks = [slab[pl.ds(pl.multiple_of(s * tile + i * 16, 16), 16), :] for s in range(slots)]
        for t in range(places):
            block = blocks[0] * weights[t][0]
            for s in range(1, slots):
                block = block + blocks[s] * weights[t][s]
            tr, tc = t // tile_cols, t % tile_cols
            at = pl.ds(pl.multiple_of(tr * tile + i * 16, 16), 16)
            dense[at, tc * tile : (tc + 1) * tile] = block[:, :tile]
            dense[at, cols + tc * tile : cols + (tc + 1) * tile] = block[:, tile:]
        return carry

    lax.fori_loop(0, tile // 16, place_rows, 0)
    loads[1].wait()
    loads[2].wait()
    third = third_t[...].astype(F32)
    halves = [dense.at[:, level * cols : (level + 1) * cols] for level in range(2)]
    first_sum = None
    for level in range(2):
        mixed = (third[level : level + 1, :] * second_t[...].astype(F32)).astype(BF16)
        term = dot(halves[level][...], mixed)
        first_sum = term if level == 0 else first_sum + term
    span = rows // rings
    first_v[...] = first_sum.reshape(rings, span, factor)
    pl.semaphore_wait(barrier, len(others))

    half = rings // 2
    cuts = [pl.ds(i * span // CUTS, span // CUTS) for i in range(CUTS)]

    def own(sign, distance):
        return (z - sign * distance + rings) % rings

    def leaf(sign, distance, hops, landing, slot):
        return [send(first_v.at[own(sign, distance), cut], landing.at[slot, cut], at_ring(-sign * hops)) for cut in cuts]

    down_runs = [leaf(1, half, 2, down_far, 0)]
    down_joins = [leaf(1, half - 1, 1, down_near, 0)]
    up_runs = [[]]
    up_joins = [leaf(-1, half - 1, 1, up_near, 0)]

    def relay(stop):
        distance = half - 2 * stop
        down_next, up_next = [], []
        for i, cut in enumerate(cuts):
            arrive([down_runs[-1][i], down_joins[-1][i]])
            down_far[stop - 1, cut] = down_far[stop - 1, cut] + down_near[stop - 1, cut] + first_v[own(1, distance), cut]
            down_next.append(send(down_far.at[stop - 1, cut], down_far.at[stop, cut], at_ring(-2)))
            up_joins[-1][i].wait_recv()
            total = up_near[stop - 1, cut] + first_v[own(-1, distance), cut]
            if stop > 1:
                up_runs[-1][i].wait_recv()
                total = total + up_far[stop - 1, cut]
            up_far[stop - 1, cut] = total
            up_next.append(send(up_far.at[stop - 1, cut], up_far.at[stop, cut], at_ring(2)))
        down_runs.append(down_next)
        up_runs.append(up_next)
        down_joins.append(leaf(1, distance - 1, 1, down_near, stop))
        up_joins.append(leaf(-1, distance - 1, 1, up_near, stop))

    loads[3].wait()
    for level in range(2):
        region[:, level * width : (level + 1) * width] = dot(halves[level][...], core_s[...]).astype(BF16)
    loads[4].wait()
    core_v[...] = dot(core_f[...], region[...]).reshape(core_v.shape)
    core_swap = send(core_v.at[:, :, 1 - core], core_c, partner)
    loads[5].wait()
    second_sum = None
    for level in range(2):
        mixed = (first_t[...].astype(F32) * third[level : level + 1, :]).astype(BF16)
        term = dot(halves[level][...], mixed, ((0,), (0,)))
        second_sum = term if level == 0 else second_sum + term
    second_v[...] = second_sum.reshape(second_v.shape)
    second_swap = send(second_v.at[:, :, 1 - core], second_c, partner)
    for level in range(2):
        across = dot(halves[level][...], second_t[...])
        third_v[0:1, level * factor : (level + 1) * factor] = jnp.sum(across * first_t[...].astype(F32), axis=0, keepdims=True)
    third_swap = send(third_v, third_c.at[core], partner)
    relay(1)

    def start_xy(total, landing):
        rows_half = total.shape[2] // 2
        copies = []
        for step in (2, 1, 3):
            to_x, to_y = (x + step) % SIDE, (y + step) % SIDE
            copies.append(send(total.at[:, to_x, 0:rows_half], landing.at[0, step - 1], at_chip(0, step)))
            copies.append(send(total.at[to_y, :, rows_half:], landing.at[1, step - 1], at_chip(step, 0)))
        return copies

    def middle_xy(total, landing, last):
        rows_half = total.shape[2] // 2
        landing[0, 0] = total[:, x, 0:rows_half] + landing[0, 0] + landing[0, 1] + landing[0, 2]
        landing[1, 0] = total[y, :, rows_half:] + landing[1, 0] + landing[1, 1] + landing[1, 2]
        copies = []
        for step in (2, 1, 3):
            to_x, to_y = (x + step) % SIDE, (y + step) % SIDE
            copies.append(send(landing.at[0, 0, to_y], last.at[0, step - 1], at_chip(step, 0)))
            copies.append(send(landing.at[1, 0, to_x], last.at[1, step - 1], at_chip(0, step)))
        return copies

    core_swap.wait_recv()
    core_c[...] = core_c[...] + core_v[:, :, core]
    core_stage = start_xy(core_c, core_1)
    relay(2)
    second_swap.wait_recv()
    second_c[...] = second_c[...] + second_v[:, :, core]
    second_stage = start_xy(second_c, second_1)
    third_swap.wait_recv()
    third_c[core] = third_v[...]
    third_xy[chip] = third_c[0] + third_c[1]
    relay(3)
    stops = half // 2
    arrive(up_runs[-1] + up_joins[-1] + down_joins[-1] + down_runs[-1])
    sketch = first_prior[...] + first_v[z] + down_near[stops - 1] + up_near[stops - 1] + up_far[stops - 1] + down_far[stops - 1]
    first_o[...] = sketch

    gram_v[...] = dot(sketch, sketch, ((0,), (0,)), HIGHEST).reshape(gram_v.shape)
    gram_swap = send(gram_v.at[1 - core], gram_c, partner)
    arrive(core_stage)
    core_last = middle_xy(core_c, core_1, core_2)
    gram_swap.wait_recv()
    gram_c[...] = gram_c[...] + gram_v[core]
    gram_stage = [
        send(gram_c.at[((y + dy) % SIDE) * SIDE + (x + dx) % SIDE], gram_xy.at[dy * SIDE + dx], at_chip(dy, dx)) for dy, dx in offsets
    ]
    arrive(second_stage)
    second_last = middle_xy(second_c, second_1, second_2)
    third_stage = [send(third_xy.at[chip], third_xy.at[chip], at_chip(*o)) for o in offsets]

    arrive(core_last)
    rows_half = core_c.shape[2] // 2
    lane = lax.broadcasted_iota(jnp.int32, (rows_half, 128), 1) // 32
    sums = [
        core_1[0, 0, y] + core_2[0, 0] + core_2[0, 1] + core_2[0, 2],
        core_1[1, 0, x] + core_2[1, 0] + core_2[1, 1] + core_2[1, 2],
    ]
    for group in range(width // 128):
        parts = [sums[k // 2][:, (k % 2) * width + group * 128 : (k % 2) * width + (group + 1) * 128] for k in range(4)]
        for m in range(4):
            piece = None
            for k in range(4):
                shift = (k - m) * 32 % 128
                moved = pltpu.roll(parts[k], shift, 1) if shift else parts[k]
                piece = moved if k == 0 else jnp.where(lane == k, moved, piece)
            pieces[group * 4 + m] = piece
    share_stage = [send(pieces.at[(z + s) % rings], pieces_in.at[s], at_ring(s)) for s in ring_order(rings)]

    arrive(gram_stage)
    total = gram_c[chip]
    for i in range(1, chips):
        total = total + gram_xy[i]
    gram_own[...] = total
    gram_ring = [send(gram_own, gram_z.at[s], at_ring(s)) for s in ring_order(rings)]
    arrive(third_stage)
    third_sum = third_xy[0]
    for i in range(1, chips):
        third_sum = third_sum + third_xy[i]
    third_z[z] = third_sum
    third_last = [send(third_z.at[z], third_z.at[z], at_ring(s)) for s in ring_order(rings)]
    arrive(second_last)
    rows_half = second_c.shape[2] // 2
    second_o[0:rows_half, :] = second_prior[0:rows_half, :] + (second_1[0, 0, y] + second_2[0, 0] + second_2[0, 1] + second_2[0, 2])
    second_o[rows_half:, :] = second_prior[rows_half:, :] + (second_1[1, 0, x] + second_2[1, 0] + second_2[1, 1] + second_2[1, 2])
    arrive(share_stage)
    share = pieces[z]
    for i in range(1, rings):
        share = share + pieces_in[i]
    share_o[...] = share
    arrive(gram_ring)
    for i in range(1, rings):
        total = total + gram_z[i]
    gram_done[core, chip] = total
    gram_spread = [send(gram_done.at[core, chip], gram_done.at[core, chip], at_chip(*o)) for o in offsets]
    arrive(third_last)
    third_sum = third_z[0]
    for i in range(1, rings):
        third_sum = third_sum + third_z[i]
    third_o[...] = third_sum
    arrive(gram_spread)
    gram_back = send(gram_done.at[core], gram_done.at[core], partner)
    gram_back.wait_recv()
    gram_o[...] = gram_done[...].reshape(gram_o.shape)
    for copy in send.copies:
        copy.wait_send()


def all_sums(slot_tiles, live_counts, slab, first_t, second_t, third_t, core_f, core_s, first_prior, second_prior):
    vmem, hbm = (pl.BlockSpec(memory_space=m) for m in (pltpu.VMEM, pl.ANY))
    rows, cols, factor, width = first_t.shape[0], second_t.shape[0], first_t.shape[1], core_s.shape[1]
    rings = lax.axis_size("col")
    chips = SIDE * SIDE
    owned, high = second_prior.shape[0], core_f.shape[0] // lax.axis_size("row")
    span = rows // rings
    half = rings // 2

    def f32(*shape):
        return pltpu.VMEM(shape, F32)

    scratch = [
        pltpu.SMEM(slot_tiles.shape, jnp.int32), pltpu.SMEM(live_counts.shape, jnp.int32),
        *(pltpu.VMEM(a.shape, BF16) for a in (slab, first_t, second_t, third_t, core_f, core_s)),
        pltpu.VMEM((rows, 2 * cols), BF16), pltpu.VMEM((rows, 2 * width), BF16),
        f32(rings, span, factor), f32(SIDE, SIDE, 2, owned, factor), f32(SIDE, SIDE, 2, high, 2 * width), f32(1, 2 * factor),
        *(f32(half // 2, span, factor) for _ in range(4)),
        f32(SIDE, SIDE, owned, factor), f32(SIDE, SIDE, high, 2 * width), f32(2, 1, 2 * factor),
        f32(2, SIDE - 1, SIDE, owned // 2, factor), f32(2, SIDE - 1, SIDE, high // 2, 2 * width),
        f32(2, SIDE - 1, owned // 2, factor), f32(2, SIDE - 1, high // 2, 2 * width),
        f32(chips, 1, 2 * factor), f32(rings, 1, 2 * factor),
        f32(2, chips, 8, factor), f32(chips, 8, factor), f32(chips, 8, factor), f32(8, factor), f32(rings, 8, factor),
        f32(2, chips, 8, factor), f32(rings, 8, 128), f32(rings, 8, 128),
        pltpu.SemaphoreType.DMA((8,)), pltpu.SemaphoreType.DMA((160,)), pltpu.SemaphoreType.DMA((160,)),
    ]
    shapes = (first_prior.shape, second_prior.shape, (1, 2 * factor), (factor, factor), (8, 128))
    return pl.pallas_call(
        sums_kernel,
        out_shape=[jax.ShapeDtypeStruct(s, F32) for s in shapes],
        in_specs=[hbm] * 8 + [vmem] * 2,
        out_specs=[vmem] * 5,
        scratch_shapes=scratch,
        compiler_params=pltpu.CompilerParams(collective_id=0, has_side_effects=True, vmem_limit_bytes=60 * 2**20),
    )(slot_tiles, live_counts, slab, first_t, second_t, third_t, core_f, core_s, first_prior, second_prior)


def eliminate(work, reciprocals, size, wide=64, group=16):
    lanes = size // 128

    def across(value):
        return jnp.concatenate([value] * lanes, axis=1)

    for start in range(0, size, wide):
        panel = work[start : start + wide, :]
        finished = []
        inverses = []
        for base in range(0, wide, group):
            high = wide - base
            at = start + base
            row_at = lax.broadcasted_iota(jnp.int32, (high, 128), 0)
            row_low = lax.broadcasted_iota(jnp.int32, (high, size), 0)
            lane_low = lax.broadcasted_iota(jnp.int32, (high, size), 1) - at
            group_row = lax.broadcasted_iota(jnp.int32, (group, 128), 0)
            inverse = jnp.zeros((group, 128), F32)
            columns = [jnp.broadcast_to(panel[:, at + k : at + k + 1], (high, 128)) for k in range(group)]
            taken = jnp.logical_and(lane_low >= 0, lane_low < group)
            panel = jnp.where(taken, jnp.where(lane_low == row_low, 1.0, 0.0), panel)
            for k in range(0, group, 2):
                one, two = columns[k], columns[k + 1]
                a, b, d = one[k : k + 1, :], two[k : k + 1, :], two[k + 1 : k + 2, :]
                inverse_one = 1.0 / a
                inverse_two = a / (a * d - b * b)
                inverse = jnp.where(group_row == k, inverse_one, jnp.where(group_row == k + 1, inverse_two, inverse))
                factor_one = jnp.where(row_at > k, one * inverse_one, 0.0)
                factor_two = jnp.where(row_at > k + 1, (two - factor_one * b) * inverse_two, 0.0)
                for later in range(k + 2, group):
                    value = columns[later] - factor_one * columns[later][k : k + 1, :]
                    columns[later] = value - factor_two * value[k + 1 : k + 2, :]
                panel = panel - across(factor_one) * panel[k : k + 1, :]
                panel = panel - across(factor_two) * panel[k + 1 : k + 2, :]
            finished.append(panel[:group])
            inverses.append(inverse)
            panel = panel[group:]
        panel = jnp.concatenate(finished, axis=0)
        inverse = jnp.concatenate(inverses, axis=0)
        reciprocals[start : start + wide, :] = inverse
        row_full = lax.broadcasted_iota(jnp.int32, (wide, size), 0)
        lane_full = lax.broadcasted_iota(jnp.int32, (wide, size), 1) - start
        panel = jnp.where(lane_full > row_full, jnp.where(lane_full < wide, 0.0, panel), panel)
        work[start : start + wide, :] = panel
        rest = size - start - wide
        if rest:
            inside = jnp.logical_and(lane_full >= 0, lane_full < wide)
            scaled = jnp.where(inside, panel, 0.0) * across(inverse)
            step = dot(scaled, panel, ((0,), (0,)), HIGHEST)
            below = work[start + wide :, :]
            lane_rest = lax.broadcasted_iota(jnp.int32, (rest, size), 1) - start
            inside_rest = jnp.logical_and(lane_rest >= 0, lane_rest < wide)
            change = dot(jnp.where(inside_rest, below, 0.0), step, precision=HIGHEST)
            work[start + wide :, :] = jnp.where(inside_rest, 0.0, below) - change


def inverse_factor(gram, work, reciprocals):
    size = gram.shape[0]
    row = lax.broadcasted_iota(jnp.int32, (size, size), 0)
    lane = lax.broadcasted_iota(jnp.int32, (size, size), 1)
    whole = gram[...]
    diagonal = jnp.where(row == lane, whole, 0.0)
    along = lax.rsqrt(jnp.sum(diagonal, axis=0, keepdims=True))
    work[...] = jnp.where(row == lane, 1.0, whole * along * lax.rsqrt(jnp.sum(diagonal, axis=1, keepdims=True)))
    eliminate(work, reciprocals, size, WIDE, GROUP)
    scale = jnp.concatenate([jnp.sqrt(reciprocals[...])] * (size // 128), axis=1)
    return jnp.where(lane <= row, work[...], 0.0) * scale * along


def basis_kernel(
    gram, sketch, second, third, share, core_t, sketch_o, second_o, third_o, update_o, basis, work, reciprocals, update, sem
):
    turned = share[...].T
    core_rows = core_t[...].astype(F32).T
    for p in range(16):
        high, low = divmod(p, 8)
        lower = turned[high * 64 : high * 64 + 32, low : low + 1] * core_rows[0:1, :]
        update[p] = lower + turned[high * 64 + 32 : high * 64 + 64, low : low + 1] * core_rows[1:2, :]
    store = pltpu.make_async_copy(update, update_o, sem)
    store.start()
    factor = third_o.shape[1]
    sketch_o[...] = sketch[...]
    second_o[...] = second[...]
    third_o[0:1, :] = third[:, :factor]
    third_o[1:2, :] = third[:, factor:]
    basis[...] = dot(sketch[...], inverse_factor(gram, work, reciprocals), ((1,), (1,)), HIGHEST)
    store.wait()


def basis_of(gram, sketch, second, third, share, core_t):
    vmem, hbm = pl.BlockSpec(memory_space=pltpu.VMEM), pl.BlockSpec(memory_space=pl.ANY)
    update = (16, 32, core_t.shape[0])
    shapes = (sketch.shape, second.shape, (2, third.shape[1] // 2), update, sketch.shape)
    return pl.pallas_call(
        basis_kernel,
        out_shape=[jax.ShapeDtypeStruct(s, F32) for s in shapes],
        in_specs=[vmem] * 6,
        out_specs=[vmem, vmem, vmem, hbm, vmem],
        scratch_shapes=[
            pltpu.VMEM(gram.shape, F32), pltpu.VMEM((gram.shape[0], 128), F32), pltpu.VMEM(update, F32), pltpu.SemaphoreType.DMA,
        ],
    )(gram, sketch, second, third, share, core_t)


def body(slab, slot_tiles, live_counts, first_prior, second_prior, first_t, second_t, third_t, core_f, core_s, core_t):
    first_sums, second_sums, third_sums, gram, share = all_sums(
        slot_tiles, live_counts, slab, first_t, second_t, third_t, core_f, core_s, first_prior, second_prior
    )
    first_sketch, second_sketch, third_sketch, core_update, first_basis = basis_of(
        gram, first_sums, second_sums, third_sums, share, core_t
    )
    return (first_sketch, second_sketch, third_sketch, core_update, first_basis)


def solution(mesh):
    both, swapped = P(("row", "col"), None), P(("col", "row"), None)
    return jax.shard_map(
        body,
        mesh=mesh,
        in_specs=(
            P("row", "col"), P("row", "col"), P("row", "col"), both, swapped,
            P("row", None), P("col", None), P(), P(None, "row"), P("col", None), P(),
        ),
        out_specs=(both, swapped, P(), P("row", "col", None), both),
        check_vma=False,
    )
```

time: 92.2 us -> 75.8 us (0.82)
  Pallas kernels: 83.4 us -> 71.4 us
  local copies, waits for them, and re-layouts: 5.19 us -> 2.82 us
  other arithmetic: 1.91 us -> 0 us
    pallas_call x1, Pallas kernels: 68.5 us -> 60.6 us  [all_sums(): pl.pallas_call(sums_kernel, out_shape=[jax.ShapeDtypeStruct(s, F32) for s...]
    pallas_call x1, Pallas kernels: 14.9 us -> 10.8 us  [basis_of(): pl.pallas_call(basis_kernel, out_shape=[jax.ShapeDtypeStruct(s, F32) for...]
    pallas_call x1 -> x0, other arithmetic: 1.32 us -> none  [all_sums(): pl.pallas_call(sums_kernel, out_shape=[jax.ShapeDtypeStruct(s, F32) for s...]
    unnamed x5 -> x2, local copies, waits for them, and re-layouts: 4.08 us -> 2.82 us
where the time goes in v3:
time: 75.8 us; the launch traced here: 75.5 us
  Pallas kernels  71.4 us (94%)
  local copies, waits for them, and re-layouts  2.82 us (4%)
  between operations  1.29 us (2%)
    pallas_call x1, Pallas kernels, all_sums(): pl.pallas_call(sums_kernel, out_shape=[jax.ShapeDtypeStruct(s, F32) for s...  60.6 us
    pallas_call x1, Pallas kernels, basis_of(): pl.pallas_call(basis_kernel, out_shape=[jax.ShapeDtypeStruct(s, F32) for...  10.8 us
    unnamed x2, local copies, waits for them, and re-layouts  2.82 us

profile of v3, /device:TPU:1, one launch (start us, length us, event | category | flops | bytes accessed | tf_op | source)
XLA Modules:
  0.0 75.5 jit_solution(16489115906206741387)
XLA Ops:
  1.3 1.3 %copy.16.tiles_h = s32[6,1]{1,0:T(8,128)} copy(s32[6,1]{0,1:T(1,128)} %param.12) | data formatting | bytes 48 | tf_op args[1]
  2.6 1.5 %copy.17.core_t = bf16[512,2]{1,0:T(8,128)(2,1)} copy(bf16[512,2]{0,1:T(2,128)(2,1)} %param.21) | data formatting | bytes 4096 | tf_op args[10]
  4.1 60.6 %shard_map.146 = (f32[32,256]{1,0:T(8,128)}, f32[32,256]{1,0:T(8,128)}, f32[1,512]{1,0:T(1,128)}, f32[256,256]{1,0:T(8,128)}, f32[8,128]{1,0:T(8,128)}) custom-call(s32[6,1]{1,0:T(8,128)} %copy.16.tiles_h, s32[1,1]{1,0:T(1,128)S(6)} %copy.18.live_h, bf16[1536,512]{1,0:T(8,128)(2,1)} %slab_h.1, bf16[512,256]{1,0:T(8,128)(2,1)} %first_h.1, ...), custom_call_target="tpu_custom_call" | custom-call | tf_op jit(solution)/shard_map/pallas_call | solution.py:320
  64.7 10.8 %shard_map.147 = (f32[32,256]{1,0:T(8,128)}, f32[32,256]{1,0:T(8,128)}, f32[2,256]{1,0:T(2,128)}, f32[16,32,512]{2,1,0:T(8,128)}, f32[32,256]{1,0:T(8,128)}) custom-call(f32[256,256]{1,0:T(8,128)} %get-tuple-element.10.gram, f32[32,256]{1,0:T(8,128)} %get-tuple-element.11.sketch, f32[32,256]{1,0:T(8,128)} %get-tuple-element.12.second, ...), custom_call_target="tpu_custom_call" | custom-call | tf_op jit(solution)/shard_map/pallas_call | solution.py:423

commit v4 on v3

--- a/solution.py
+++ b/solution.py
@@ -50,7 +50,7 @@
 def sums_kernel(
     tiles_h, live_h, slab_h, first_h, second_h, third_h, core_f_h, core_s_h, first_prior, second_prior,
     first_o, second_o, third_o, gram_o, share_o,
-    tiles_ref, live_ref, slab, first_t, second_t, third_t, core_f, core_s, dense, region,
+    tiles_ref, live_ref, slab, first_t, second_t, third_t, core_f, core_s, mixed, dense, region,
     first_v, second_v, core_v, third_v, down_far, down_near, up_far, up_near, second_c, core_c, third_c,
     second_1, core_1, second_2, core_2, third_xy, third_z,
     gram_v, gram_c, gram_xy, gram_own, gram_z, gram_done, pieces, pieces_in,
@@ -69,14 +69,14 @@
     y, x = chip // SIDE, chip % SIDE
     chips = SIDE * SIDE
 
-    loads = [
-        pltpu.make_async_copy(source, target, load_sems.at[i])
-        for i, (source, target) in enumerate(
-            ((slab_h, slab), (third_h, third_t), (second_h, second_t), (core_s_h, core_s), (core_f_h, core_f), (first_h, first_t), (tiles_h, tiles_ref), (live_h, live_ref))
-        )
-    ]
-    for load in loads[6:] + loads[:6]:
-        load.start()
+    def load(source, target, at):
+        return pltpu.make_async_copy(source, target, load_sems.at[at])
+
+    early = [load(third_h, third_t, 0), load(second_h, second_t, 1), load(tiles_h, tiles_ref, 2), load(live_h, live_ref, 3)]
+    blocks_in = [load(slab_h.at[s * tile : (s + 1) * tile], slab.at[s * tile : (s + 1) * tile], 4 + s) for s in range(slots)]
+    late = [load(core_s_h, core_s, 4 + slots), load(core_f_h, core_f, 5 + slots), load(first_h, first_t, 6 + slots)]
+    for copy in early + blocks_in + late:
+        copy.start()
 
     def at_chip(dy, dx):
         return ((((y + dy) % SIDE) * SIDE + (x + dx) % SIDE) * 2 + core, z)
@@ -90,43 +90,35 @@
         key=lambda o: -(min(o[0], SIDE - o[0]) + min(o[1], SIDE - o[1])),
     )
     barrier = pltpu.get_barrier_semaphore()
-    others = [partner] + [at_chip(*o) for o in offsets if not (o[0] and o[1])] + [at_ring(s) for s in (-2, -1, 1, 2)]
+    others = [partner] + [at_chip(*o) for o in offsets] + [at_ring(s) for s in (-2, -1, 1, 2)]
     for device in others:
         pl.semaphore_signal(barrier, inc=1, device_id=device, device_id_type=MESH)
 
     send = Sender(send_sems, recv_sems)
-    loads[6].wait()
-    loads[7].wait()
+    early[0].wait()
+    early[1].wait()
+    third = third_t[...].astype(F32)
+    for level in range(2):
+        mixed[level] = (third[level : level + 1, :] * second_t[...].astype(F32)).astype(BF16)
+    early[2].wait()
+    early[3].wait()
     live = live_ref[0, 0]
     places = (rows // tile) * tile_cols
     weights = [
-        [jnp.logical_and(tiles_ref[s, 0] == t, s < live).astype(jnp.int32).astype(F32).astype(BF16) for s in range(slots)]
+        [jnp.logical_and(tiles_ref[0, s] == t, s < live).astype(jnp.int32).astype(F32).astype(BF16) for s in range(slots)]
         for t in range(places)
     ]
-    loads[0].wait()
-
-    def place_rows(i, carry):
-        blocks = [slab[pl.ds(pl.multiple_of(s * tile + i * 16, 16), 16), :] for s in range(slots)]
-        for t in range(places):
-            block = blocks[0] * weights[t][0]
-            for s in range(1, slots):
-                block = block + blocks[s] * weights[t][s]
-            tr, tc = t // tile_cols, t % tile_cols
-            at = pl.ds(pl.multiple_of(tr * tile + i * 16, 16), 16)
-            dense[at, tc * tile : (tc + 1) * tile] = block[:, :tile]
-            dense[at, cols + tc * tile : cols + (tc + 1) * tile] = block[:, tile:]
-        return carry
-
-    lax.fori_loop(0, tile // 16, place_rows, 0)
-    loads[1].wait()
-    loads[2].wait()
-    third = third_t[...].astype(F32)
+    for copy in blocks_in:
+        copy.wait()
+    for t in range(places):
+        block = slab[0:tile, :] * weights[t][0]
+        for s in range(1, slots):
+            block = block + slab[s * tile : (s + 1) * tile, :] * weights[t][s]
+        at, tc = pl.ds(t // tile_cols * tile, tile), t % tile_cols
+        dense[at, tc * tile : (tc + 1) * tile] = block[:, :tile]
+        dense[at, cols + tc * tile : cols + (tc + 1) * tile] = block[:, tile:]
     halves = [dense.at[:, level * cols : (level + 1) * cols] for level in range(2)]
-    first_sum = None
-    for level in range(2):
-        mixed = (third[level : level + 1, :] * second_t[...].astype(F32)).astype(BF16)
-        term = dot(halves[level][...], mixed)
-        first_sum = term if level == 0 else first_sum + term
+    first_sum = dot(halves[0][...], mixed[0]) + dot(halves[1][...], mixed[1])
     span = rows // rings
     first_v[...] = first_sum.reshape(rings, span, factor)
     pl.semaphore_wait(barrier, len(others))
@@ -164,17 +156,17 @@
         down_joins.append(leaf(1, distance - 1, 1, down_near, stop))
         up_joins.append(leaf(-1, distance - 1, 1, up_near, stop))
 
-    loads[3].wait()
+    late[0].wait()
     for level in range(2):
         region[:, level * width : (level + 1) * width] = dot(halves[level][...], core_s[...]).astype(BF16)
-    loads[4].wait()
+    late[1].wait()
     core_v[...] = dot(core_f[...], region[...]).reshape(core_v.shape)
     core_swap = send(core_v.at[:, :, 1 - core], core_c, partner)
-    loads[5].wait()
+    late[2].wait()
     second_sum = None
     for level in range(2):
-        mixed = (first_t[...].astype(F32) * third[level : level + 1, :]).astype(BF16)
-        term = dot(halves[level][...], mixed, ((0,), (0,)))
+        weights = (first_t[...].astype(F32) * third[level : level + 1, :]).astype(BF16)
+        term = dot(halves[level][...], weights, ((0,), (0,)))
         second_sum = term if level == 0 else second_sum + term
     second_v[...] = second_sum.reshape(second_v.shape)
     second_swap = send(second_v.at[:, :, 1 - core], second_c, partner)
@@ -222,16 +214,29 @@
 
     gram_v[...] = dot(sketch, sketch, ((0,), (0,)), HIGHEST).reshape(gram_v.shape)
     gram_swap = send(gram_v.at[1 - core], gram_c, partner)
-    arrive(core_stage)
-    core_last = middle_xy(core_c, core_1, core_2)
     gram_swap.wait_recv()
     gram_c[...] = gram_c[...] + gram_v[core]
     gram_stage = [
         send(gram_c.at[((y + dy) % SIDE) * SIDE + (x + dx) % SIDE], gram_xy.at[dy * SIDE + dx], at_chip(dy, dx)) for dy, dx in offsets
     ]
+    arrive(core_stage)
+    core_last = middle_xy(core_c, core_1, core_2)
     arrive(second_stage)
     second_last = middle_xy(second_c, second_1, second_2)
     third_stage = [send(third_xy.at[chip], third_xy.at[chip], at_chip(*o)) for o in offsets]
+
+    arrive(gram_stage)
+    total = gram_c[chip]
+    for i in range(1, chips):
+        total = total + gram_xy[i]
+    gram_own[...] = total
+    gram_ring = [send(gram_own, gram_z.at[s], at_ring(s)) for s in ring_order(rings)]
+    arrive(third_stage)
+    third_sum = third_xy[0]
+    for i in range(1, chips):
+        third_sum = third_sum + third_xy[i]
+    third_z[z] = third_sum
+    third_last = [send(third_z.at[z], third_z.at[z], at_ring(s)) for s in ring_order(rings)]
 
     arrive(core_last)
     rows_half = core_c.shape[2] // 2
@@ -250,40 +255,28 @@
                 piece = moved if k == 0 else jnp.where(lane == k, moved, piece)
             pieces[group * 4 + m] = piece
     share_stage = [send(pieces.at[(z + s) % rings], pieces_in.at[s], at_ring(s)) for s in ring_order(rings)]
-
-    arrive(gram_stage)
-    total = gram_c[chip]
-    for i in range(1, chips):
-        total = total + gram_xy[i]
-    gram_own[...] = total
-    gram_ring = [send(gram_own, gram_z.at[s], at_ring(s)) for s in ring_order(rings)]
-    arrive(third_stage)
-    third_sum = third_xy[0]
-    for i in range(1, chips):
-        third_sum = third_sum + third_xy[i]
-    third_z[z] = third_sum
-    third_last = [send(third_z.at[z], third_z.at[z], at_ring(s)) for s in ring_order(rings)]
     arrive(second_last)
     rows_half = second_c.shape[2] // 2
     second_o[0:rows_half, :] = second_prior[0:rows_half, :] + (second_1[0, 0, y] + second_2[0, 0] + second_2[0, 1] + second_2[0, 2])
     second_o[rows_half:, :] = second_prior[rows_half:, :] + (second_1[1, 0, x] + second_2[1, 0] + second_2[1, 1] + second_2[1, 2])
+
+    arrive(gram_ring)
+    for i in range(1, rings):
+        total = total + gram_z[i]
+    gram_done[core, chip] = total
+    gram_spread = [send(gram_done.at[core, chip], gram_done.at[core, chip], at_chip(*o)) for o in offsets]
+    arrive(gram_spread)
+    gram_back = send(gram_done.at[core], gram_done.at[core], partner)
     arrive(share_stage)
     share = pieces[z]
     for i in range(1, rings):
         share = share + pieces_in[i]
     share_o[...] = share
-    arrive(gram_ring)
-    for i in range(1, rings):
-        total = total + gram_z[i]
-    gram_done[core, chip] = total
-    gram_spread = [send(gram_done.at[core, chip], gram_done.at[core, chip], at_chip(*o)) for o in offsets]
     arrive(third_last)
     third_sum = third_z[0]
     for i in range(1, rings):
         third_sum = third_sum + third_z[i]
     third_o[...] = third_sum
-    arrive(gram_spread)
-    gram_back = send(gram_done.at[core], gram_done.at[core], partner)
     gram_back.wait_recv()
     gram_o[...] = gram_done[...].reshape(gram_o.shape)
     for copy in send.copies:
@@ -305,7 +298,7 @@
     scratch = [
         pltpu.SMEM(slot_tiles.shape, jnp.int32), pltpu.SMEM(live_counts.shape, jnp.int32),
         *(pltpu.VMEM(a.shape, BF16) for a in (slab, first_t, second_t, third_t, core_f, core_s)),
-        pltpu.VMEM((rows, 2 * cols), BF16), pltpu.VMEM((rows, 2 * width), BF16),
+        pltpu.VMEM((2, *second_t.shape), BF16), pltpu.VMEM((rows, 2 * cols), BF16), pltpu.VMEM((rows, 2 * width), BF16),
         f32(rings, span, factor), f32(SIDE, SIDE, 2, owned, factor), f32(SIDE, SIDE, 2, high, 2 * width), f32(1, 2 * factor),
         *(f32(half // 2, span, factor) for _ in range(4)),
         f32(SIDE, SIDE, owned, factor), f32(SIDE, SIDE, high, 2 * width), f32(2, 1, 2 * factor),
@@ -314,7 +307,7 @@
         f32(chips, 1, 2 * factor), f32(rings, 1, 2 * factor),
         f32(2, chips, 8, factor), f32(chips, 8, factor), f32(chips, 8, factor), f32(8, factor), f32(rings, 8, factor),
         f32(2, chips, 8, factor), f32(rings, 8, 128), f32(rings, 8, 128),
-        pltpu.SemaphoreType.DMA((8,)), pltpu.SemaphoreType.DMA((160,)), pltpu.SemaphoreType.DMA((160,)),
+        pltpu.SemaphoreType.DMA((16,)), pltpu.SemaphoreType.DMA((160,)), pltpu.SemaphoreType.DMA((160,)),
     ]
     shapes = (first_prior.shape, second_prior.shape, (1, 2 * factor), (factor, factor), (8, 128))
     return pl.pallas_call(
@@ -325,6 +318,12 @@
         scratch_shapes=scratch,
         compiler_params=pltpu.CompilerParams(collective_id=0, has_side_effects=True, vmem_limit_bytes=60 * 2**20),
     )(slot_tiles, live_counts, slab, first_t, second_t, third_t, core_f, core_s, first_prior, second_prior)
+
+
+def block_lanes(rows, start, wide):
+    shift = start % 128
+    value = rows[:, start - shift : start - shift + 128]
+    return (pltpu.roll(value, 128 - shift, 1) if shift else value)[:, :wide]
 
 
 def eliminate(work, reciprocals, size, wide=64, group=16):
@@ -352,7 +351,7 @@
                 one, two = columns[k], columns[k + 1]
                 a, b, d = one[k : k + 1, :], two[k : k + 1, :], two[k + 1 : k + 2, :]
                 inverse_one = 1.0 / a
-                inverse_two = a / (a * d - b * b)
+                inverse_two = a * (1.0 / (a * d - b * b))
                 inverse = jnp.where(group_row == k, inverse_one, jnp.where(group_row == k + 1, inverse_two, inverse))
                 factor_one = jnp.where(row_at > k, one * inverse_one, 0.0)
                 factor_two = jnp.where(row_at > k + 1, (two - factor_one * b) * inverse_two, 0.0)
@@ -374,13 +373,12 @@
         rest = size - start - wide
         if rest:
             inside = jnp.logical_and(lane_full >= 0, lane_full < wide)
-            scaled = jnp.where(inside, panel, 0.0) * across(inverse)
+            scaled = block_lanes(panel, start, wide) * inverse[:, :wide]
             step = dot(scaled, panel, ((0,), (0,)), HIGHEST)
-            below = work[start + wide :, :]
-            lane_rest = lax.broadcasted_iota(jnp.int32, (rest, size), 1) - start
-            inside_rest = jnp.logical_and(lane_rest >= 0, lane_rest < wide)
-            change = dot(jnp.where(inside_rest, below, 0.0), step, precision=HIGHEST)
-            work[start + wide :, :] = jnp.where(inside_rest, 0.0, below) - change
+            for low in range(start + wide, size, wide):
+                below = work[low : low + wide, :]
+                change = dot(block_lanes(below, start, wide), step, precision=HIGHEST)
+                work[low : low + wide, :] = jnp.where(inside, 0.0, below) - change
 
 
 def inverse_factor(gram, work, reciprocals):
@@ -400,7 +398,7 @@
     gram, sketch, second, third, share, core_t, sketch_o, second_o, third_o, update_o, basis, work, reciprocals, update, sem
 ):
     turned = share[...].T
-    core_rows = core_t[...].astype(F32).T
+    core_rows = core_t[...].astype(F32)
     for p in range(16):
         high, low = divmod(p, 8)
         lower = turned[high * 64 : high * 64 + 32, low : low + 1] * core_rows[0:1, :]
@@ -418,7 +416,7 @@
 
 def basis_of(gram, sketch, second, third, share, core_t):
     vmem, hbm = pl.BlockSpec(memory_space=pltpu.VMEM), pl.BlockSpec(memory_space=pl.ANY)
-    update = (16, 32, core_t.shape[0])
+    update = (16, 32, core_t.shape[1])
     shapes = (sketch.shape, second.shape, (2, third.shape[1] // 2), update, sketch.shape)
     return pl.pallas_call(
         basis_kernel,
@@ -433,10 +431,10 @@
 
 def body(slab, slot_tiles, live_counts, first_prior, second_prior, first_t, second_t, third_t, core_f, core_s, core_t):
     first_sums, second_sums, third_sums, gram, share = all_sums(
-        slot_tiles, live_counts, slab, first_t, second_t, third_t, core_f, core_s, first_prior, second_prior
+        slot_tiles.T, live_counts, slab, first_t, second_t, third_t, core_f, core_s, first_prior, second_prior
     )
     first_sketch, second_sketch, third_sketch, core_update, first_basis = basis_of(
-        gram, first_sums, second_sums, third_sums, share, core_t
+        gram, first_sums, second_sums, third_sums, share, core_t.T
     )
     return (first_sketch, second_sketch, third_sketch, core_update, first_basis)
 

time: 75.8 us -> 69.5 us (0.917)
  Pallas kernels: 71.4 us -> 68 us
  local copies, waits for them, and re-layouts: 2.82 us -> 0 us
    unnamed x2 -> x0, local copies, waits for them, and re-layouts: 2.82 us -> none
    pallas_call x1, Pallas kernels: 60.6 us -> 58.3 us  [all_sums(): pl.pallas_call(sums_kernel, out_shape=[jax.ShapeDtypeStruct(s, F32) for s...]
    pallas_call x1, Pallas kernels: 10.8 us -> 9.67 us  [basis_of(): pl.pallas_call(basis_kernel, out_shape=[jax.ShapeDtypeStruct(s, F32) for...]
where the time goes in v4:
time: 69.5 us; the launch traced here: 69.3 us
  Pallas kernels  68 us (98%)
  between operations  1.29 us (2%)
    pallas_call x1, Pallas kernels, all_sums(): pl.pallas_call(sums_kernel, out_shape=[jax.ShapeDtypeStruct(s, F32) for s...  58.3 us
    pallas_call x1, Pallas kernels, basis_of(): pl.pallas_call(basis_kernel, out_shape=[jax.ShapeDtypeStruct(s, F32) for...  9.67 us

profile of v4, /device:TPU:1, one launch (start us, length us, event | category | flops | bytes accessed | tf_op | source)
XLA Modules:
  0.0 69.3 jit_solution(923826385125618379)
XLA Ops:
  1.3 58.3 %shard_map.146 = (f32[32,256]{1,0:T(8,128)}, f32[32,256]{1,0:T(8,128)}, f32[1,512]{1,0:T(1,128)}, f32[256,256]{1,0:T(8,128)}, f32[8,128]{1,0:T(8,128)}) custom-call(s32[1,6]{1,0:T(1,128)} %bitcast.3, s32[1,1]{1,0:T(1,128)S(6)} %copy.16.live_h, bf16[1536,512]{1,0:T(8,128)(2,1)} %slab_h.1, bf16[512,256]{1,0:T(8,128)(2,1)} %first_h.1, ...), custom_call_target="tpu_custom_call" | custom-call | tf_op jit(solution)/shard_map/pallas_call | solution.py:313
  59.6 9.7 %shard_map.147 = (f32[32,256]{1,0:T(8,128)}, f32[32,256]{1,0:T(8,128)}, f32[2,256]{1,0:T(2,128)}, f32[16,32,512]{2,1,0:T(8,128)}, f32[32,256]{1,0:T(8,128)}) custom-call(f32[256,256]{1,0:T(8,128)} %get-tuple-element.10.gram, f32[32,256]{1,0:T(8,128)} %get-tuple-element.11.sketch, f32[32,256]{1,0:T(8,128)} %get-tuple-element.12.second, ...), custom_call_target="tpu_custom_call" | custom-call | tf_op jit(solution)/shard_map/pallas_call | solution.py:421

commit v5 on v4

--- a/solution.py
+++ b/solution.py
@@ -206,6 +206,7 @@
     third_swap.wait_recv()
     third_c[core] = third_v[...]
     third_xy[chip] = third_c[0] + third_c[1]
+    third_stage = [send(third_xy.at[chip], third_xy.at[chip], at_chip(*o)) for o in offsets]
     relay(3)
     stops = half // 2
     arrive(up_runs[-1] + up_joins[-1] + down_joins[-1] + down_runs[-1])
@@ -219,11 +220,16 @@
     gram_stage = [
         send(gram_c.at[((y + dy) % SIDE) * SIDE + (x + dx) % SIDE], gram_xy.at[dy * SIDE + dx], at_chip(dy, dx)) for dy, dx in offsets
     ]
+    arrive(third_stage)
+    third_sum = third_xy[0]
+    for i in range(1, chips):
+        third_sum = third_sum + third_xy[i]
+    third_z[z] = third_sum
+    third_last = [send(third_z.at[z], third_z.at[z], at_ring(s)) for s in ring_order(rings)]
     arrive(core_stage)
     core_last = middle_xy(core_c, core_1, core_2)
     arrive(second_stage)
     second_last = middle_xy(second_c, second_1, second_2)
-    third_stage = [send(third_xy.at[chip], third_xy.at[chip], at_chip(*o)) for o in offsets]
 
     arrive(gram_stage)
     total = gram_c[chip]
@@ -231,12 +237,6 @@
         total = total + gram_xy[i]
     gram_own[...] = total
     gram_ring = [send(gram_own, gram_z.at[s], at_ring(s)) for s in ring_order(rings)]
-    arrive(third_stage)
-    third_sum = third_xy[0]
-    for i in range(1, chips):
-        third_sum = third_sum + third_xy[i]
-    third_z[z] = third_sum
-    third_last = [send(third_z.at[z], third_z.at[z], at_ring(s)) for s in ring_order(rings)]
 
     arrive(core_last)
     rows_half = core_c.shape[2] // 2

time: 69.5 us -> 69.3 us (level)
  no operation moved by 1% of the time
where the time goes in v5:
time: 69.3 us; the launch traced here: 69 us
  Pallas kernels  67.8 us (98%)
  between operations  1.29 us (2%)
    pallas_call x1, Pallas kernels, all_sums(): pl.pallas_call(sums_kernel, out_shape=[jax.ShapeDtypeStruct(s, F32) for s...  58.1 us
    pallas_call x1, Pallas kernels, basis_of(): pl.pallas_call(basis_kernel, out_shape=[jax.ShapeDtypeStruct(s, F32) for...  9.67 us

profile of v5, /device:TPU:1, one launch (start us, length us, event | category | flops | bytes accessed | tf_op | source)
XLA Modules:
  0.0 69.0 jit_solution(14942554560950089242)
XLA Ops:
  1.3 58.1 %shard_map.146 = (f32[32,256]{1,0:T(8,128)}, f32[32,256]{1,0:T(8,128)}, f32[1,512]{1,0:T(1,128)}, f32[256,256]{1,0:T(8,128)}, f32[8,128]{1,0:T(8,128)}) custom-call(s32[1,6]{1,0:T(1,128)} %bitcast.3, s32[1,1]{1,0:T(1,128)S(6)} %copy.16.live_h, bf16[1536,512]{1,0:T(8,128)(2,1)} %slab_h.1, bf16[512,256]{1,0:T(8,128)(2,1)} %first_h.1, ...), custom_call_target="tpu_custom_call" | custom-call | tf_op jit(solution)/shard_map/pallas_call | solution.py:313
  59.4 9.7 %shard_map.147 = (f32[32,256]{1,0:T(8,128)}, f32[32,256]{1,0:T(8,128)}, f32[2,256]{1,0:T(2,128)}, f32[16,32,512]{2,1,0:T(8,128)}, f32[32,256]{1,0:T(8,128)}) custom-call(f32[256,256]{1,0:T(8,128)} %get-tuple-element.10.gram, f32[32,256]{1,0:T(8,128)} %get-tuple-element.11.sketch, f32[32,256]{1,0:T(8,128)} %get-tuple-element.12.second, ...), custom_call_target="tpu_custom_call" | custom-call | tf_op jit(solution)/shard_map/pallas_call | solution.py:421
